TPU v7x, 32 devices: a whole 2x2x4 slice. The times are simulated.
32 devices in a mesh: leaf: 8 (over z, x), helper: 4 (over y, core).
Axes of the slice: x: 2, y: 2, z: 4, core: 2. Of those that a mesh axis runs over, the one named last changes fastest.
Arguments:
- charges: bfloat16 [32, 262144], P(None, ('leaf', 'helper')), may hold values from -6 to 6
- leaf_basis: bfloat16 [2048, 64, 128], P(('leaf', 'helper')), may hold values from -0.5 to 0.5
- near_field: bfloat16 [2048, 128, 128], P(('leaf', 'helper')), may hold values from -0.5 to 0.5
- local_transfer: bfloat16 [8, 510, 4096], P('leaf'), may hold values from -0.625 to 0.625
- top_transfer: bfloat16 [14, 4096], replicated, may hold values from -0.625 to 0.625
- top_coupling: bfloat16 [14, 4096], replicated, may hold values from -0.75 to 0.75
- leaf_coupling: bfloat16 [8, 4096, 64, 64], P('leaf', 'helper'), may hold values from -0.75 to 0.75
- task_target: int32 [8, 4096], P('leaf', 'helper'), may hold values from 0 to 256, as said below
- task_source: int32 [8, 4096], P('leaf', 'helper'), may hold values from 0 to 767, as said below
Outputs:
- potential: bfloat16 [32, 262144], P(None, ('leaf', 'helper'))
Inputs may be any that keep to these rules, and one draw needn't show every extreme that they name: `task_target`: on every device of helper the live slots (target below 256) come first and the others hold target 256; each subtree has exactly 2048 live slots, and one device of each subtree has all 1024 of its slots live. `task_source`: A live slot's source names a leaf of an existing subtree: k * 256 + leaf with k = 0 for the previous subtree, 1 for its own, 2 for the next; empty slots hold 0.
All inputs are finite; a program needn't handle non-finite values.
Results may differ from a plain program's by a relative error of at most 0.0058.
Values may be sent and summed in bfloat16 or wider, within the bound.
No kernel may reach another device: no remote copies, remote signals or barrier semaphores. Data moves between devices by JAX's collectives and lax.ppermute only.
A program may use at most 192 MiB of HBM per device.

v0:
```python
import jax
import jax.numpy as jnp
from jax import lax
from jax.sharding import PartitionSpec as P

RANK = 64
RHS = 32
LEAF = 128


highest = lax.Precision.HIGHEST


def with_halo(shard, sides, width):
    for axis, dim in sides:
        count, length = (lax.axis_size(axis), shard.shape[dim])
        up = [(i, (i + 1) % count) for i in range(count - 1)]
        down = [(j, i) for i, j in up]
        last = lax.slice_in_dim(shard, length - width, length, axis=dim)
        initial = lax.slice_in_dim(shard, 0, width, axis=dim)
        before = lax.ppermute(last, axis, up)
        after = lax.ppermute(initial, axis, down)
        shard = jnp.concatenate([before, shard, after], axis=dim)
    return shard


def partner_2(block, axis, bit):
    count = lax.axis_size(axis)
    route = []
    for low in range(count):
        high = low | 1 << bit
        if high != low and high < count:
            route += [(low, high), (high, low)]
    return lax.ppermute(block, axis, route)


def couple_tasks(blocks, targets, sources, window, group_leaves):
    picked = window[sources]
    products = jnp.einsum("tij,tjr->tir", blocks, picked, preferred_element_type=jnp.float32)
    selector = jax.nn.one_hot(targets, group_leaves, dtype=jnp.float32)
    return jnp.einsum("ts,tir->sir", selector, products, precision=highest)


def shards(
    charges,
    leaf_basis,
    near_field,
    local_transfer,
    top_transfer,
    top_coupling,
    leaf_coupling,
    task_target,
    task_source,
):
    helpers = lax.axis_size("helper")
    groups = lax.axis_size("leaf")
    helper_index = lax.axis_index("helper")
    group_index = lax.axis_index("leaf")
    own_leaves = leaf_basis.shape[0]
    group_leaves = own_leaves * helpers
    points = charges.reshape(RHS, own_leaves, LEAF)
    own_coef = jnp.einsum(
        "lkp,rlp->lkr", leaf_basis, points, preferred_element_type=jnp.float32
    ).astype(jnp.bfloat16)
    group_coef = lax.all_gather(own_coef, "helper", axis=0, tiled=True)
    window = with_halo(group_coef, (("leaf", 0),), group_leaves)
    partial_value = couple_tasks(
        leaf_coupling[0], task_target[0], task_source[0], window, group_leaves
    )
    coupling_own = lax.psum_scatter(partial_value, "helper", scatter_dimension=0, tiled=True)
    local_mats = local_transfer[0]
    current = own_coef.astype(jnp.float32)
    offset = 0
    nodes_now = group_leaves
    local_levels = []
    while nodes_now > 1:
        if nodes_now == helpers:
            current = lax.all_gather(current, "helper", axis=0, tiled=True)
        if nodes_now > helpers:
            wanted = nodes_now // helpers
            matrices = lax.dynamic_slice_in_dim(
                local_mats, offset + helper_index * wanted, wanted, 0
            )
        else:
            wanted = nodes_now
            matrices = local_mats[offset : offset + nodes_now]
        matrices = matrices.astype(jnp.float32).reshape(wanted, RANK, RANK)
        lifted = jnp.einsum("nij,nir->njr", matrices, current, precision=highest)
        current = lifted.reshape(wanted // 2, 2, RANK, RHS).sum(axis=1)
        local_levels.append((offset, nodes_now))
        offset = offset + nodes_now
        nodes_now = nodes_now // 2
    group_root = current[0]
    top_matrices = top_transfer.reshape(2 * groups - 2, RANK, RANK)
    top_links = top_coupling.reshape(2 * groups - 2, RANK, RANK)
    levels_up = groups.bit_length() - 1
    own_value = group_root
    received = []
    own_moves = []
    for height in range(levels_up):
        partner = partner_2(own_value, "leaf", height)
        offset = 2 * groups - 2 * (groups >> height)
        node_index = jnp.right_shift(group_index, height)
        sibling_node = jnp.bitwise_xor(node_index, 1)
        own_move = lax.dynamic_index_in_dim(
            top_matrices, offset + node_index, 0, keepdims=False
        ).astype(jnp.float32)
        other_move = lax.dynamic_index_in_dim(
            top_matrices, offset + sibling_node, 0, keepdims=False
        ).astype(jnp.float32)
        link_matrix = lax.dynamic_index_in_dim(
            top_links, offset + node_index, 0, keepdims=False
        ).astype(jnp.float32)
        received.append(jnp.dot(link_matrix, partner, precision=highest))
        own_moves.append(own_move)
        own_value = jnp.dot(own_move.T, own_value, precision=highest) + jnp.dot(
            other_move.T, partner, precision=highest
        )
    group_down = received[-1]
    for height in range(levels_up - 2, -1, -1):
        group_down = received[height] + jnp.dot(own_moves[height], group_down, precision=highest)
    downward = group_down[None]
    first_node = 0
    length = 1
    for offset, nodes_now in reversed(local_levels):
        repeated = jnp.repeat(downward, 2, axis=0)
        first_node = first_node * 2
        length = length * 2
        if nodes_now >= helpers and length > nodes_now // helpers:
            wanted = nodes_now // helpers
            own_first = helper_index * wanted
            repeated = lax.dynamic_slice_in_dim(repeated, own_first - first_node, wanted, 0)
            first_node = own_first
            length = wanted
        matrices = (
            lax.dynamic_slice_in_dim(local_mats, offset + first_node, length, 0)
            .astype(jnp.float32)
            .reshape(length, RANK, RANK)
        )
        downward = jnp.einsum("nij,njr->nir", matrices, repeated, precision=highest)
    leaf_field = (coupling_own + downward).astype(jnp.bfloat16)
    far_part = jnp.einsum(
        "lkp,lkr->rlp", leaf_basis, leaf_field, preferred_element_type=jnp.float32
    )
    near_part = jnp.einsum("lpq,rlq->rlp", near_field, points, preferred_element_type=jnp.float32)
    return (far_part + near_part).astype(jnp.bfloat16).reshape(RHS, own_leaves * LEAF)


def solution(mesh):
    return jax.shard_map(
        shards,
        mesh=mesh,
        in_specs=(
            P(None, ("leaf", "helper")),
            P(("leaf", "helper"), None, None),
            P(("leaf", "helper"), None, None),
            P("leaf", None, None),
            P(),
            P(),
            P("leaf", "helper", None, None),
            P("leaf", "helper"),
            P("leaf", "helper"),
        ),
        out_specs=P(None, ("leaf", "helper")),
        check_vma=False,
    )
```

profile of v0, /device:TPU:0, one launch (start us, length us, event | category | flops | bytes accessed | tf_op | source)
XLA Modules:
  0.0 214.6 jit_solution(9812416511275049168)
XLA Ops:
  6.5 3.0 %convolution_convert_fusion = bf16[64,64,32]{1,2,0:T(8,128)(2,1)} fusion(bf16[64,64,128]{2,1,0:T(8,128)(2,1)} %param.10, bf16[32,8192]{1,0:T(8,128)(2,1)} %param.9), kind=kOutput, calls=%fused_computation.7 | convolution fusion | flops 33685504 | bytes 1835008 | tf_op jit(solution)/shard_map/lkp,rlp->lkr/dot_general | solution.py:62
  9.6 2.0 constant_dynamic-slice_fusion.5
  16.8 2.1 reshape.158
  28.7 6.3 %all-gather.4.cloned.1.call-done = bf16[256,64,32]{1,2,0:T(8,128)(2,1)} async-done(((bf16[64,64,32]{1,2,0:T(8,128)(2,1)}), bf16[256,64,32]{1,2,0:T(8,128)(2,1)}) %all-gather.4.cloned.1.call-update) | async-done | bytes 1048592 | tf_op jit(solution)/shard_map/all_gather | solution.py:65
  35.0 4.9 %copy.20 = bf16[256,64,32]{0,2,1:T(8,128)(2,1)} copy(bf16[256,64,32]{1,2,0:T(8,128)(2,1)} %all-gather.4.cloned.1.call-done) | data formatting | bytes 2097152 | tf_op jit(solution)/shard_map/all_gather | solution.py:65
  39.9 4.4 %collective-permute-start = (bf16[256,64,32]{0,2,1:T(8,128)(2,1)}, bf16[256,64,32]{0,2,1:T(8,128)(2,1)}, u32[]{:S(2)}, u32[]{:S(2)}) collective-permute-start(bf16[256,64,32]{0,2,1:T(8,128)(2,1)} %copy.20), channel_id=1, source_target_pairs={{0,4},{4,8},{8,12},{12,16},{16,20},{20,24},{24,28},{1,5},{5,9},{9,... | collective-permute-start | bytes 3145736 | tf_op jit(solution)/shard_map/ppermute | solution.py:21
  51.7 5.4 %all-gather.1 = f32[4,64,32]{1,2,0:T(8,128)S(1)} all-gather(f32[1,64,32]{1,2,0:T(8,128)S(1)} %convolution_bitcast_fusion.2), channel_id=2, replica_groups=mesh['leaf'=8,'helper'=4] {'helper'}, dimensions={0}, use_global_device_ids=true | all-gather | bytes 40960 | tf_op jit(solution)/shard_map/all_gather | solution.py:78
  59.1 2.7 %collective-permute-start.2 = (f32[64,32]{0,1:T(8,128)S(1)}, f32[64,32]{0,1:T(8,128)}, u32[]{:S(2)}, u32[]{:S(2)}) collective-permute-start(f32[64,32]{0,1:T(8,128)S(1)} %bitcast.135), channel_id=1, source_target_pairs={{0,4},{4,0},{8,12},{12,8},{16,20},{20,16},{24,28},{28,24},{1,5},{5... | collective-permute-start | bytes 24584 | tf_op jit(solution)/shard_map/ppermute | solution.py:34
  61.8 1.8 reshape.174
  63.6 23.9 %copy.24 = bf16[1024,64,64]{2,1,0:T(8,128)(2,1)} copy(bf16[1024,64,64]{0,2,1:T(8,128)(2,1)} %bitcast.128) | data formatting | bytes 16777216 | tf_op jit(solution)/shard_map/squeeze | solution.py:68
  89.0 5.4 %copy.22 = bf16[256,64,32]{1,2,0:T(8,128)(2,1)} copy(bf16[256,64,32]{0,2,1:T(8,128)(2,1)} %collective-permute-done) | data formatting | bytes 2097152 | tf_op jit(solution)/shard_map/ppermute | solution.py:21
  94.4 5.4 %copy.23 = bf16[256,64,32]{1,2,0:T(8,128)(2,1)} copy(bf16[256,64,32]{0,2,1:T(8,128)(2,1)} %collective-permute-done.1) | data formatting | bytes 2097152 | tf_op jit(solution)/shard_map/ppermute | solution.py:22
  99.7 6.4 %pad_maximum_fusion = bf16[768,64,32]{1,2,0:T(8,128)(2,1)} fusion(bf16[256,64,32]{1,2,0:T(8,128)(2,1)} %copy.23, bf16[256,64,32]{1,2,0:T(8,128)(2,1)} %all-gather.4.cloned.1.call-done, bf16[256,64,32]{1,2,0:T(8,128)(2,1)} %copy.22), kind=kLoop, calls=%fused_computation.4 | loop fusion | flops 3145728 | bytes 6291456 | tf_op jit(solution)/shard_map/concatenate | solution.py:23
  106.1 12.7 %gather_fusion = bf16[1024,64,32]{1,2,0:T(8,128)(2,1)} fusion(bf16[768,64,32]{1,2,0:T(8,128)(2,1)} %pad_maximum_fusion, s32[1024]{0:T(1024)} %broadcast_clamp_fusion), kind=kCustom, calls=%fused_computation | custom fusion | bytes 8392704 | tf_op jit(solution)/shard_map/gather | solution.py:38
  118.8 19.3 %convolution_bitcast_fusion = f32[1024,64,32]{1,2,0:T(8,128)} fusion(bf16[1024,64,32]{1,2,0:T(8,128)(2,1)} %gather_fusion, bf16[1024,64,64]{2,1,0:T(8,128)(2,1)} %copy.24), kind=kOutput, calls=%fused_computation.3 | convolution fusion | flops 268435456 | bytes 20971520 | tf_op jit(solution)/shard_map/tij,tjr->tir/dot_general | solution.py:39
  138.2 19.7 %fusion = f32[256,64,32]{1,0,2:T(8,128)} fusion(f32[1024,64,32]{1,2,0:T(8,128)} %convolution_bitcast_fusion, s32[1024]{0:T(1024)S(1)} %bitcast.137), kind=kOutput, calls=%fused_computation.1 | convolution fusion | flops 6442713088 | bytes 10489856 | tf_op jit(solution)/shard_map/ts,tir->sir/dot_general | solution.py:41
  165.5 2.4 %collective-permute-start.4 = (f32[64,32]{0,1:T(8,128)}, f32[64,32]{0,1:T(8,128)}, u32[]{:S(2)}, u32[]{:S(2)}) collective-permute-start(f32[64,32]{0,1:T(8,128)} %convolution_add_fusion.1), channel_id=1, source_target_pairs={{0,16},{16,0},{4,20},{20,4},{8,24},{24,8},{12,28},{28,12},{1,17},{... | collective-permute-start | bytes 24584 | tf_op jit(solution)/shard_map/ppermute | solution.py:34
  167.9 3.3 %fusion.7 = f32[64,32,128]{2,1,0:T(8,128)} fusion(bf16[64,128,128]{2,1,0:T(8,128)(2,1)S(1)} %copy-done, bf16[32,8192]{1,0:T(8,128)(2,1)} %param.9), kind=kOutput, calls=%fused_computation.21 | convolution fusion | flops 67108864 | bytes 3670016 | tf_op jit(solution)/shard_map/lpq,rlq->rlp/dot_general | solution.py:145
  171.2 1.8 reshape.165
  186.8 2.0 fusion.60
  188.9 2.8 %fusion.61 = f32[64,64,32]{1,2,0:T(8,128)} fusion(bf16[64,64,64]{2,1,0:T(8,128)(2,1)S(1)} %reshape.158, f32[64,64,32]{1,2,0:T(8,128)S(1)} %bitcast.129), kind=kOutput, calls=%fused_computation.89 | convolution fusion | flops 100663296 | bytes 1572864 | tf_op jit(solution)/shard_map/nij,njr->nir/dot_general | solution.py:140
  191.7 10.9 %reduce-scatter.2.cloned.1.call-done = f32[64,64,32]{1,0,2:T(8,128)} async-done(((f32[256,64,32]{1,0,2:T(8,128)}), f32[64,64,32]{1,0,2:T(8,128)}) %reduce-scatter.2.cloned.1.call-update) | async-done | bytes 524304 | tf_op jit(solution)/shard_map/reduce_scatter | solution.py:70
  202.6 2.2 %fusion.4 = bf16[64,64,32]{1,0,2:T(8,128)(2,1)S(1)} fusion(f32[64,64,32]{1,0,2:T(8,128)} %reduce-scatter.2.cloned.1.call-done, f32[64,64,32]{1,2,0:T(8,128)} %fusion.61), kind=kLoop, calls=%fused_computation.17 | loop fusion | flops 262144 | bytes 1310720 | tf_op jit(solution)/shard_map/convert_element_type | solution.py:141
  204.7 2.1 %fusion.3 = bf16[64,4,8,128]{3,2,1,0:T(8,128)(2,1)S(1)} fusion(f32[64,32,128]{2,1,0:T(8,128)} %fusion.7, bf16[64,64,128]{2,1,0:T(8,128)(2,1)} %param.10, bf16[64,64,32]{1,0,2:T(8,128)(2,1)S(1)} %fusion.4), kind=kOutput, calls=%fused_computation.8 | convolution fusion | flops 34078720 | bytes 2883584 | tf_op jit(solution)/shard_map/lkp,lkr->rlp/dot_general | solution.py:142
  (64 shorter events, 48.3 us)
Async XLA Ops:
  6.5 161.4 %copy-start = (bf16[64,128,128]{2,1,0:T(8,128)(2,1)S(1)}, bf16[64,128,128]{2,1,0:T(8,128)(2,1)}, u32[]{:S(2)}) copy-start(bf16[64,128,128]{2,1,0:T(8,128)(2,1)} %param.11) | copy-start | bytes 6291460
  6.5 28.4 %all-gather.4.cloned.1.call-start = ((), (), s32[]{:S(2)}) async-start(), calls=%async_computation.1 | async-start | bytes 2621440 | tf_op jit(solution)/shard_map/all_gather | solution.py:65
  9.5 193.0 %reduce-scatter.2.cloned.1.call-start = ((), (), s32[]{:S(2)}) async-start(), calls=%async_computation.2 | async-start | bytes 5242880 | tf_op jit(solution)/shard_map/reduce_scatter | solution.py:70
  39.9 49.1 %collective-permute-start = (bf16[256,64,32]{0,2,1:T(8,128)(2,1)}, bf16[256,64,32]{0,2,1:T(8,128)(2,1)}, u32[]{:S(2)}, u32[]{:S(2)}) collective-permute-start(bf16[256,64,32]{0,2,1:T(8,128)(2,1)} %copy.20), channel_id=1, source_target_pairs={{0,4},{4,8},{8,12},{12,16},{16,20},{20,24},{24,28},{1,5},{5,9},{9,... | collective-permute-start | bytes 3145736 | tf_op jit(solution)/shard_map/ppermute | solution.py:21
  44.2 50.2 %collective-permute-start.1 = (bf16[256,64,32]{0,2,1:T(8,128)(2,1)}, bf16[256,64,32]{0,2,1:T(8,128)(2,1)}, u32[]{:S(2)}, u32[]{:S(2)}) collective-permute-start(bf16[256,64,32]{0,2,1:T(8,128)(2,1)} %copy.20), channel_id=1, source_target_pairs={{4,0},{8,4},{12,8},{16,12},{20,16},{24,20},{28,24},{5,1},{9,5},{13... | collective-permute-start | bytes 3145736 | tf_op jit(solution)/shard_map/ppermute | solution.py:22
  59.1 100.2 %collective-permute-start.2 = (f32[64,32]{0,1:T(8,128)S(1)}, f32[64,32]{0,1:T(8,128)}, u32[]{:S(2)}, u32[]{:S(2)}) collective-permute-start(f32[64,32]{0,1:T(8,128)S(1)} %bitcast.135), channel_id=1, source_target_pairs={{0,4},{4,0},{8,12},{12,8},{16,20},{20,16},{24,28},{28,24},{1,5},{5... | collective-permute-start | bytes 24584 | tf_op jit(solution)/shard_map/ppermute | solution.py:34
  118.8 19.3 %copy-start.2 = (s32[1,1024]{1,0:T(1,128)S(1)}, s32[1,1024]{1,0:T(1,128)}, u32[]{:S(2)}) copy-start(s32[1,1024]{1,0:T(1,128)} %param.16) | copy-start | bytes 12292
  160.2 3.8 %collective-permute-start.3 = (f32[64,32]{0,1:T(8,128)S(1)}, f32[64,32]{0,1:T(8,128)S(1)}, u32[]{:S(2)}, u32[]{:S(2)}) collective-permute-start(f32[64,32]{0,1:T(8,128)S(1)} %convolution_add_fusion.3), channel_id=1, source_target_pairs={{0,8},{8,0},{4,12},{12,4},{16,24},{24,16},{20,28},{28,20},{1,9},{9... | collective-permute-start | bytes 24584 | tf_op jit(solution)/shard_map/ppermute | solution.py:34
  164.0 1.5 copy-start.1
  165.5 9.8 %collective-permute-start.4 = (f32[64,32]{0,1:T(8,128)}, f32[64,32]{0,1:T(8,128)}, u32[]{:S(2)}, u32[]{:S(2)}) collective-permute-start(f32[64,32]{0,1:T(8,128)} %convolution_add_fusion.1), channel_id=1, source_target_pairs={{0,16},{16,0},{4,20},{20,4},{8,24},{24,8},{12,28},{28,12},{1,17},{... | collective-permute-start | bytes 24584 | tf_op jit(solution)/shard_map/ppermute | solution.py:34
Sparse Core Ops, SparseCore 0:
  9.6 25.2 all-gather.3
  158.0 44.5 reduce-scatter.1
where the time goes:
time: 217 us; the launch traced here: 215 us
  local copies, waits for them, and re-layouts  80.1 us (37%)
  matrix products  74.5 us (34%)
  waiting for transfers between devices  18.7 us (9%)
  between operations  13.6 us (6%)
  starting transfers between devices  12.3 us (6%)
  other arithmetic  9.86 us (5%)
  blocking collectives  5.42 us (2%)
    squeeze x1, local copies, waits for them, and re-layouts, shards(): leaf_coupling[0]  23.9 us
    dot_general x1, matrix products, couple_tasks(): return jnp.einsum('ts,tir->sir', selector, products, precision=highest)  19.7 us
    dot_general x1, matrix products, couple_tasks(): jnp.einsum('tij,tjr->tir', blocks, picked, preferred_element_type=jnp.flo...  19.3 us
    gather x1, local copies, waits for them, and re-layouts, couple_tasks(): picked = window[sources]  12.7 us
    reduce_scatter x1, waiting for transfers between devices, shards(): lax.psum_scatter(partial_value, 'helper', scatter_dimension=0, tiled=True)  10.9 us
    dot_general x8, matrix products, shards(): downward = jnp.einsum('nij,njr->nir', matrices, repeated, precision=highest)  9.26 us
    dot_general x8, matrix products, shards(): lifted = jnp.einsum('nij,nir->njr', matrices, current, precision=highest)  8.8 us
    dynamic_slice x6, local copies, waits for them, and re-layouts, shards(): lax.dynamic_slice_in_dim(local_mats, offset + first_node, length, 0)  8.56 us
  transfers between devices with their start and end apart: 7, of which 4 were waited for; matrix products, arithmetic and copies ran while one was open for 71% of the time, Pallas kernels for 0%

commit v1 on v0

v1 whole, which is shorter than its diff:
```python
import functools

import jax
import jax.numpy as jnp
from jax import lax
from jax.experimental import pallas as pl
from jax.experimental.pallas import tpu as pltpu
from jax.sharding import PartitionSpec as P

BF = jnp.bfloat16
F32 = jnp.float32
NT = (((1,), (1,)), ((), ()))
NN = (((1,), (0,)), ((), ()))
BLOCK = 128
STEP = 8


def dot(a, b, dims=NN):
    return lax.dot_general(a, b, dims, preferred_element_type=F32)


def cost(flops, size):
    return pl.CostEstimate(flops=flops, bytes_accessed=size, transcendentals=0)


def lane_low(shape, width):
    return lax.broadcasted_iota(jnp.int32, shape, 1) < width


def split_rows(value):
    high = value.astype(BF)
    low = (value - high.astype(F32)).astype(BF)
    return jnp.concatenate([high, low], axis=0)


def precise(value, matrix, dims=NN):
    rows = value.shape[0]
    both = dot(split_rows(value), matrix, dims)
    return both[:rows] + both[rows:]


def coef_kernel(x_ref, basis_ref, out_ref):
    pairs, rhs, wide = out_ref.shape
    leaf = basis_ref.shape[-1]
    low = lane_low((rhs, wide), wide // 2)
    for p in range(pairs):
        first = x_ref[:, 2 * p * leaf : (2 * p + 1) * leaf]
        second = x_ref[:, (2 * p + 1) * leaf : (2 * p + 2) * leaf]
        both = dot(jnp.concatenate([first, second], axis=0), basis_ref[p], NT)
        out_ref[p] = jnp.where(low, both[:rhs], both[rhs:]).astype(BF)


def leaf_coefs(charges, basis_pairs):
    rhs = charges.shape[0]
    pairs, wide, leaf = basis_pairs.shape
    steps = 4
    per = pairs // steps
    return pl.pallas_call(
        coef_kernel,
        grid=(steps,),
        out_shape=jax.ShapeDtypeStruct((pairs, rhs, wide), BF),
        in_specs=[
            pl.BlockSpec((rhs, per * 2 * leaf), lambda b: (0, b)),
            pl.BlockSpec((per, wide, leaf), lambda b: (b, 0, 0)),
        ],
        out_specs=pl.BlockSpec((per, rhs, wide), lambda b: (b, 0, 0)),
        cost_estimate=cost(pairs * 2 * rhs * wide * leaf * 2, 2_000_000),
        name="coefs",
    )(charges, basis_pairs)


def near_kernel(x_ref, near_ref, out_ref):
    leaf = near_ref.shape[-1]
    for k in range(near_ref.shape[0]):
        here = slice(k * leaf, (k + 1) * leaf)
        out_ref[:, here] = dot(x_ref[:, here], near_ref[k], NT)


def near_part(charges, near_field):
    rhs = charges.shape[0]
    leaves, leaf, _ = near_field.shape
    steps = 4
    per = leaves // steps
    return pl.pallas_call(
        near_kernel,
        grid=(steps,),
        out_shape=jax.ShapeDtypeStruct(charges.shape, F32),
        in_specs=[
            pl.BlockSpec((rhs, per * leaf), lambda b: (0, b)),
            pl.BlockSpec((per, leaf, leaf), lambda b: (b, 0, 0)),
        ],
        out_specs=pl.BlockSpec((rhs, per * leaf), lambda b: (0, b)),
        cost_estimate=cost(leaves * rhs * leaf * leaf * 2, 4_000_000),
        name="near",
    )(charges, near_field)


def turn_kernel(in_ref, out_ref, turned):
    rank = in_ref.shape[0]
    tasks = in_ref.shape[2]
    row = lax.broadcasted_iota(jnp.int32, (tasks, tasks), 0)
    col = lax.broadcasted_iota(jnp.int32, (tasks, tasks), 1)
    unit = (row == col).astype(BF)

    @pl.loop(0, rank, step=8)
    def _(start):
        for k in range(8):
            slab = in_ref[start + k]
            twice = jnp.concatenate([slab, slab], axis=0)
            turned[pl.ds(start + k, tasks, stride=rank), :] = dot(unit, twice, NT)

    out_ref[...] = turned[...].astype(BF).reshape(out_ref.shape)


def turn_blocks(blocks):
    rank, _, slots = blocks.shape
    wide = 2 * rank
    return pl.pallas_call(
        turn_kernel,
        grid=(slots // BLOCK,),
        out_shape=jax.ShapeDtypeStruct((slots, rank, wide), BF),
        in_specs=[pl.BlockSpec((rank, rank, BLOCK), lambda b: (0, 0, b))],
        out_specs=pl.BlockSpec((BLOCK, rank, wide), lambda b: (b, 0, 0)),
        scratch_shapes=[pltpu.VMEM((BLOCK * rank, wide), F32)],
        cost_estimate=cost(slots * rank * wide * 256, 24_000_000),
        name="turn",
    )(blocks)


def task_kernel(parts, live_ref, source_ref, target_ref, *rest):
    window_refs = rest[:parts]
    blocks_ref, own_ref, rest_ref, window, sums, sems = rest[parts:]
    pairs, rhs, wide = window_refs[0].shape
    rank = wide // 2
    step = pl.program_id(0)
    tasks = blocks_ref.shape[0]
    copies = [
        pltpu.make_async_copy(ref, window.at[pl.ds(k * pairs, pairs)], sems.at[k])
        for k, ref in enumerate(window_refs)
    ]

    @pl.when(step == 0)
    def _():
        for copy in copies:
            copy.start()
        sums[...] = jnp.zeros_like(sums)
        for copy in copies:
            copy.wait()

    low = lane_low((rhs, wide), rank)
    base = step * tasks
    count = jnp.clip(live_ref[0] - base, 0, tasks)

    @pl.loop(0, (count + STEP - 1) // STEP)
    def _(group):
        found = []
        for k in range(STEP):
            slot = group * STEP + k
            source = source_ref[base + slot]
            pair = window[lax.shift_right_logical(source, 1)]
            keep = low == ((source & 1) == 0)
            lhs = jnp.where(keep, pair, jnp.zeros_like(pair))
            found.append(dot(lhs, blocks_ref[slot], NT))
        for k in range(STEP):
            slot = group * STEP + k
            sums[target_ref[base + slot]] += found[k]

    @pl.when(step == pl.num_programs(0) - 1)
    def _():
        def joined(p):
            return jnp.concatenate([sums[2 * p], sums[2 * p + 1]], axis=1)

        @pl.loop(0, own_ref.shape[0])
        def _(p):
            own_ref[p] = joined(p)

        @pl.loop(0, rest_ref.shape[0])
        def _(p):
            rest_ref[p] = joined(p + own_ref.shape[0]).astype(BF)


def couple(windows, turned, live, sources, targets, group_leaves, own_pairs):
    parts = len(windows)
    pairs, rhs, wide = windows[0].shape
    slots, rank, _ = turned.shape
    rest = group_leaves // 2 - own_pairs
    whole = lambda b, *_: (0, 0, 0)
    grid_spec = pltpu.PrefetchScalarGridSpec(
        num_scalar_prefetch=3,
        grid=(slots // BLOCK,),
        in_specs=[pl.BlockSpec(memory_space=pl.ANY)] * parts
        + [pl.BlockSpec((BLOCK, rank, wide), lambda b, *_: (b, 0, 0))],
        out_specs=[
            pl.BlockSpec((own_pairs, rhs, wide), whole),
            pl.BlockSpec((rest, rhs, wide), whole),
        ],
        scratch_shapes=[
            pltpu.VMEM((parts * pairs, rhs, wide), BF),
            pltpu.VMEM((group_leaves + 8, rhs, rank), F32),
            pltpu.SemaphoreType.DMA((parts,)),
        ],
    )
    return pl.pallas_call(
        functools.partial(task_kernel, parts),
        grid_spec=grid_spec,
        out_shape=[
            jax.ShapeDtypeStruct((own_pairs, rhs, wide), F32),
            jax.ShapeDtypeStruct((rest, rhs, wide), BF),
        ],
        cost_estimate=cost(slots * rhs * rank * wide * 16, 24_000_000),
        name="tasks",
    )(live, sources, targets, *windows, turned)


def up_kernel(coef_ref, mats_ref, top_ref):
    pairs = coef_ref.shape[0]
    nodes = [dot(coef_ref[p], mats_ref[p]) for p in range(pairs)]
    offset = pairs
    while len(nodes) > 1:
        joined = [
            jnp.concatenate([nodes[2 * p], nodes[2 * p + 1]], axis=1)
            for p in range(len(nodes) // 2)
        ]
        nodes = [precise(j, mats_ref[offset + p]) for p, j in enumerate(joined)]
        offset += len(nodes)
    top_ref[...] = nodes[0]


def tree_up(coefs, mats):
    _, rhs, wide = coefs.shape
    return pl.pallas_call(
        up_kernel,
        out_shape=jax.ShapeDtypeStruct((rhs, wide // 2), F32),
        cost_estimate=cost(mats.size * rhs * 16, 2 * mats.size),
        name="up",
    )(coefs, mats)


def root_kernel(nodes_ref, mats_ref, helper_ref, root_ref):
    helper = helper_ref[0]
    nodes = [nodes_ref[k] for k in range(nodes_ref.shape[0])]
    offset = 0
    level = 0
    while len(nodes) > 1:
        home = lax.shift_right_logical(helper, level)
        lifted = [
            precise(node, mats_ref[offset + jnp.bitwise_xor(home, k)])
            for k, node in enumerate(nodes)
        ]
        offset += len(nodes)
        level += 1
        nodes = [lifted[2 * k] + lifted[2 * k + 1] for k in range(len(nodes) // 2)]
    root_ref[...] = nodes[0]


def group_root(nodes, mats, helper):
    _, rhs, rank = nodes.shape
    return pl.pallas_call(
        root_kernel,
        out_shape=jax.ShapeDtypeStruct((rhs, rank), F32),
        in_specs=[
            pl.BlockSpec(memory_space=pltpu.VMEM),
            pl.BlockSpec(memory_space=pltpu.VMEM),
            pl.BlockSpec(memory_space=pltpu.SMEM),
        ],
        cost_estimate=cost(mats.size * rhs * 16, 2 * mats.size),
        name="root",
    )(nodes, mats, helper)


def down_kernel(
    roots_ref, top_ref, link_ref, crown_ref, mats_ref, place_ref, out_ref
):
    group, helper = place_ref[0], place_ref[1]
    nodes = [roots_ref[k] for k in range(roots_ref.shape[0])]
    helpers = (crown_ref.shape[0] + 2) // 2
    offset = 0
    level = 0
    far = []
    moves = []
    while len(nodes) > 1:
        home = lax.shift_right_logical(group, level)
        far.append(precise(nodes[1], link_ref[offset + home], NT))
        moves.append(offset + home)
        lifted = [
            precise(node, top_ref[offset + jnp.bitwise_xor(home, k)])
            for k, node in enumerate(nodes)
        ] if len(nodes) > 2 else []
        offset += len(nodes)
        level += 1
        nodes = [lifted[2 * k] + lifted[2 * k + 1] for k in range(len(lifted) // 2)]
    down = far[-1]
    for t in range(len(far) - 2, -1, -1):
        down = far[t] + precise(down, top_ref[moves[t]], NT)
    level = helpers.bit_length() - 2
    offset = crown_ref.shape[0]
    count = 2
    while count <= helpers:
        offset -= count
        down = precise(down, crown_ref[offset + lax.shift_right_logical(helper, level)], NT)
        level -= 1
        count *= 2
    nodes = [down]
    pairs = out_ref.shape[0]
    rank = down.shape[1]
    offset = mats_ref.shape[0]
    while len(nodes) <= pairs:
        offset -= len(nodes)
        joined = [precise(node, mats_ref[offset + p], NT) for p, node in enumerate(nodes)]
        if len(nodes) == pairs:
            for p, value in enumerate(joined):
                out_ref[p] = value
            break
        nodes = [part for j in joined for part in (j[:, :rank], j[:, rank:])]


def tree_down(roots, top, links, crown, mats, place, pairs):
    _, rhs, rank = roots.shape
    vmem = pl.BlockSpec(memory_space=pltpu.VMEM)
    return pl.pallas_call(
        down_kernel,
        out_shape=jax.ShapeDtypeStruct((pairs, rhs, 2 * rank), F32),
        in_specs=[vmem] * 5 + [pl.BlockSpec(memory_space=pltpu.SMEM)],
        cost_estimate=cost(mats.size * rhs * 16, 2 * mats.size),
        name="down",
    )(roots, top, links, crown, mats, place)


def final_kernel(count, own_ref, *rest):
    added = rest[:count]
    down_ref, basis_ref, near_ref, out_ref = rest[count:]
    pairs, rhs, wide = own_ref.shape
    leaf = basis_ref.shape[-1]
    low = lane_low((rhs, wide), wide // 2)
    for p in range(pairs):
        total = own_ref[p]
        for ref in added:
            total = total + ref[p].astype(F32)
        field = (total + down_ref[p]).astype(BF)
        none = jnp.zeros_like(field)
        lhs = jnp.concatenate(
            [jnp.where(low, field, none), jnp.where(low, none, field)], axis=0
        )
        far = dot(lhs, basis_ref[p])
        for half in range(2):
            here = slice((2 * p + half) * leaf, (2 * p + half + 1) * leaf)
            out_ref[:, here] = (
                far[half * rhs : (half + 1) * rhs] + near_ref[:, here]
            ).astype(BF)


def finish(own, added, down, basis_pairs, near):
    pairs, rhs, wide = own.shape
    leaf = basis_pairs.shape[-1]
    steps = 4
    per = pairs // steps
    pair_spec = pl.BlockSpec((per, rhs, wide), lambda b: (b, 0, 0))
    flat_spec = pl.BlockSpec((rhs, per * 2 * leaf), lambda b: (0, b))
    return pl.pallas_call(
        functools.partial(final_kernel, len(added)),
        grid=(steps,),
        out_shape=jax.ShapeDtypeStruct(near.shape, BF),
        in_specs=[pair_spec] * (2 + len(added))
        + [pl.BlockSpec((per, wide, leaf), lambda b: (b, 0, 0)), flat_spec],
        out_specs=flat_spec,
        cost_estimate=cost(pairs * rhs * wide * leaf * 4, 5_000_000),
        name="final",
    )(own, *added, down, basis_pairs, near)


def xor_move(value, axis, mask):
    count = lax.axis_size(axis)
    return lax.ppermute(value, axis, [(i, i ^ mask) for i in range(count)])


def shards(
    charges,
    leaf_basis,
    near_field,
    local_transfer,
    top_transfer,
    top_coupling,
    leaf_coupling,
    task_target,
    task_source,
):
    helpers = lax.axis_size("helper")
    groups = lax.axis_size("leaf")
    helper = lax.axis_index("helper")
    group = lax.axis_index("leaf")
    own_leaves, rank, leaf = leaf_basis.shape
    group_leaves = own_leaves * helpers
    own_pairs = own_leaves // 2
    bits = helpers.bit_length() - 1

    basis_pairs = leaf_basis.reshape(own_pairs, 2 * rank, leaf)
    own = leaf_coefs(charges, basis_pairs)

    partner = xor_move(own, "leaf", 1)
    beyond = lax.ppermute(
        partner,
        "leaf",
        [(i, i + 2) for i in range(0, groups - 2, 2)]
        + [(i, i - 2) for i in range(3, groups, 2)],
    )

    def spread(block):
        blocks = {0: block}
        for bit in reversed(range(bits)):
            for k in sorted(blocks):
                blocks[k | 1 << bit] = xor_move(blocks[k], "helper", 1 << bit)
        return [blocks[k] for k in range(helpers)]

    windows = spread(own) + spread(partner) + spread(beyond)

    def place_of(leaf_index):
        owner = jnp.bitwise_xor(leaf_index // own_leaves, helper)
        return owner * own_leaves + leaf_index % own_leaves

    targets, sources = task_target[0], task_source[0]
    is_live = targets < group_leaves
    live = jnp.sum(is_live.astype(jnp.int32)).reshape(1)
    side = sources // group_leaves
    near_side = jnp.where(group % 2 == 0, 2, 0)
    slot = jnp.where(side == 1, 0, jnp.where(side == near_side, 1, 2))
    source_place = slot * group_leaves + place_of(sources % group_leaves)
    target_place = jnp.where(is_live, place_of(targets), group_leaves)

    turned = turn_blocks(jnp.transpose(leaf_coupling[0], (1, 2, 0)))
    near = near_part(charges, near_field)

    rows = local_transfer[0]
    picked = []
    offset = 0
    count = group_leaves
    while count > helpers:
        wanted = count // helpers
        picked.append(lax.dynamic_slice_in_dim(rows, offset + helper * wanted, wanted, 0))
        offset += count
        count //= 2
    mats = jnp.concatenate(picked, axis=0).reshape(own_leaves - 1, 2 * rank, rank)
    crown = rows[offset:].reshape(-1, rank, rank)
    top = top_transfer.reshape(-1, rank, rank)
    links = top_coupling.reshape(-1, rank, rank)

    def gather_nodes(node, axis, size):
        nodes = node[None]
        bit = 1
        while bit < size:
            nodes = jnp.concatenate([nodes, xor_move(nodes, axis, bit)], axis=0)
            bit *= 2
        return nodes

    top_node = tree_up(own, mats)
    root = group_root(
        gather_nodes(top_node, "helper", helpers), crown, helper.reshape(1)
    )
    roots = gather_nodes(root, "leaf", groups)
    down = tree_down(
        roots, top, links, crown, mats, jnp.stack([group, helper]), own_pairs
    )

    sums, others = couple(
        windows, turned, live, source_place, target_place, group_leaves, own_pairs
    )
    blocks = {
        k + 1: others[k * own_pairs : (k + 1) * own_pairs] for k in range(helpers - 1)
    }
    added = []
    for bit in range(bits):
        keep = [k for k in range(0, helpers, 2 << bit)]
        send = jnp.concatenate([blocks[k | 1 << bit] for k in keep], axis=0)
        got = xor_move(send, "helper", 1 << bit)
        for place, k in enumerate(keep):
            piece = got[place * own_pairs : (place + 1) * own_pairs]
            if k == 0:
                added.append(piece)
            else:
                blocks[k] = (blocks[k].astype(F32) + piece.astype(F32)).astype(BF)
    return finish(sums, added, down, basis_pairs, near)


def solution(mesh):
    return jax.shard_map(
        shards,
        mesh=mesh,
        in_specs=(
            P(None, ("leaf", "helper")),
            P(("leaf", "helper"), None, None),
            P(("leaf", "helper"), None, None),
            P("leaf", None, None),
            P(),
            P(),
            P("leaf", "helper", None, None),
            P("leaf", "helper"),
            P("leaf", "helper"),
        ),
        out_specs=P(None, ("leaf", "helper")),
        check_vma=False,
    )
```

time: 217 us -> 168 us (0.77)
  Pallas kernels: 0 us -> 90.9 us
  matrix products: 74.5 us -> 0 us
  local copies, waits for them, and re-layouts: 80.1 us -> 18.6 us
  starting transfers between devices: 12.3 us -> 30.1 us
  between operations: 13.6 us -> 0.24 us
  blocking collectives: 5.42 us -> 0 us
  other arithmetic: 9.86 us -> 7.18 us
    pallas_call x0 -> x8, Pallas kernels: none -> 90.9 us  [the longest x1 40 us: turn_blocks(): pl.pallas_call(turn_kernel, grid=(slots // BLOCK,), out_shape=jax.ShapeDt...]
    dot_general x30 -> x0, matrix products: 74.5 us -> none  [the longest x1 19.7 us: couple_tasks(): return jnp.einsum('ts,tir->sir', selector, products, precision=highest)]
    squeeze x1 -> x0, local copies, waits for them, and re-layouts: 23.9 us -> none  [shards(): leaf_coupling[0]]
    ppermute x5 -> x18, waiting for transfers between devices: 1.54 us -> 19.7 us  [the longest x17 16.7 us: xor_move(): return lax.ppermute(value, axis, [(i, i ^ mask) for i in range(count)])]
    ppermute x5 -> x18, starting transfers between devices: 12.3 us -> 30.1 us  [the longest x17 26.6 us: xor_move(): return lax.ppermute(value, axis, [(i, i ^ mask) for i in range(count)])]
    gather x1 -> x0, local copies, waits for them, and re-layouts: 12.7 us -> none  [couple_tasks(): picked = window[sources]]
    reduce_scatter x1 -> x0, waiting for transfers between devices: 10.9 us -> none  [shards(): lax.psum_scatter(partial_value, 'helper', scatter_dimension=0, tiled=True)]
    ppermute x2 -> x0, local copies, waits for them, and re-layouts: 10.8 us -> none  [the longest x1 5.38 us: with_halo(): before = lax.ppermute(last, axis, up)]
  transfers between devices with their start and end apart: 7 -> 18, of which waited for: 4 -> 8; matrix products, arithmetic and copies ran while one was open for 71% -> 14% of each run, Pallas kernels for 0% -> 33%
where the time goes in v1:
time: 168 us; the launch traced here: 167 us
  Pallas kernels  90.9 us (54%)
  starting transfers between devices  30.1 us (18%)
  waiting for transfers between devices  19.7 us (12%)
  local copies, waits for them, and re-layouts  18.6 us (11%)
  other arithmetic  7.18 us (4%)
    pallas_call x1, Pallas kernels, turn_blocks(): pl.pallas_call(turn_kernel, grid=(slots // BLOCK,), out_shape=jax.ShapeDt...  40 us
    pallas_call x1, Pallas kernels, couple(): pl.pallas_call(functools.partial(task_kernel, parts), grid_spec=grid_spec...  27.5 us
    ppermute x17, starting transfers between devices, xor_move(): return lax.ppermute(value, axis, [(i, i ^ mask) for i in range(count)])  26.6 us
    ppermute x17, waiting for transfers between devices, xor_move(): return lax.ppermute(value, axis, [(i, i ^ mask) for i in range(count)])  16.7 us
    dynamic_slice x6, local copies, waits for them, and re-layouts, shards(): lax.dynamic_slice_in_dim(rows, offset + helper * wanted, wanted, 0)  7.18 us
    pallas_call x1, Pallas kernels, tree_down(): pl.pallas_call(down_kernel, out_shape=jax.ShapeDtypeStruct((pairs, rhs, 2...  5.42 us
    pallas_call x1, Pallas kernels, near_part(): pl.pallas_call(near_kernel, grid=(steps,), out_shape=jax.ShapeDtypeStruct...  4.45 us
    concatenate x5, other arithmetic, gather_nodes(): nodes = jnp.concatenate([nodes, xor_move(nodes, axis, bit)], axis=0)  4.19 us
  transfers between devices with their start and end apart: 18, of which 8 were waited for; matrix products, arithmetic and copies ran while one was open for 14% of the time, Pallas kernels for 33%

profile of v1, /device:TPU:0, one launch (start us, length us, event | category | flops | bytes accessed | tf_op | source)
XLA Modules:
  0.0 166.7 jit_solution(149362822724359277)
XLA Ops:
  0.0 3.9 %coefs.1.rest_0_.coef_ref = bf16[32,32,128]{2,1,0:T(8,128)(2,1)} custom-call(bf16[32,8192]{1,0:T(8,128)(2,1)} %x_ref.3, bf16[32,128,128]{2,1,0:T(8,128)(2,1)} %bitcast.24), custom_call_target="tpu_custom_call" | custom-call | flops 67108864 | bytes 2000000 | tf_op jit(solution)/shard_map/coefs/pallas_call | solution.py:58
  4.4 2.5 %collective-permute-start.1 = (bf16[32,32,128]{2,1,0:T(8,128)(2,1)}, bf16[32,32,128]{2,1,0:T(8,128)(2,1)S(1)}, u32[]{:S(2)}, u32[]{:S(2)}) collective-permute-start(bf16[32,32,128]{2,1,0:T(8,128)(2,1)} %coefs.1.rest_0_.coef_ref), channel_id=1, source_target_pairs={{0,2},{1,3},{2,0},{3,1},{4,6},{5,7},{6,4},{7,5},{8,10},{9,11},{10,... | collective-permute-start | bytes 786440 | tf_op jit(solution)/shard_map/ppermute | solution.py:373
  6.9 1.5 collective-permute-start.3
  11.6 3.9 %collective-permute-done.3.rest_4_ = bf16[32,32,128]{2,1,0:T(8,128)(2,1)S(1)} collective-permute-done((bf16[32,32,128]{2,1,0:T(8,128)(2,1)}, bf16[32,32,128]{2,1,0:T(8,128)(2,1)S(1)}, u32[]{:S(2)}, u32[]{:S(2)}) %collective-permute-start.3) | collective-permute-done | bytes 262176 | tf_op jit(solution)/shard_map/ppermute | solution.py:373
  15.5 3.5 %collective-permute-start.7 = (bf16[32,32,128]{2,1,0:T(8,128)(2,1)S(1)}, bf16[32,32,128]{2,1,0:T(8,128)(2,1)S(1)}, u32[]{:S(2)}, u32[]{:S(2)}) collective-permute-start(bf16[32,32,128]{2,1,0:T(8,128)(2,1)S(1)} %collective-permute-done.3.rest_4_), channel_id=1, source_target_pairs={{0,8},{8,16},{16,24},{12,4},{20,12},{28,20},{1,9},{9,17},{17,25},{... | collective-permute-start | bytes 786440 | tf_op jit(solution)/shard_map/ppermute | solution.py:400
  19.0 1.6 dynamic-slice_bitcast_fusion.3
  21.1 3.0 %collective-permute-done.7.rest_8_ = bf16[32,32,128]{2,1,0:T(8,128)(2,1)S(1)} collective-permute-done((bf16[32,32,128]{2,1,0:T(8,128)(2,1)S(1)}, bf16[32,32,128]{2,1,0:T(8,128)(2,1)S(1)}, u32[]{:S(2)}, u32[]{:S(2)}) %collective-permute-start.7) | collective-permute-done | bytes 262176 | tf_op jit(solution)/shard_map/ppermute | solution.py:400
  24.6 1.5 dynamic-slice_bitcast_fusion.4
  26.8 3.0 %collective-permute-done.5.rest_6_ = bf16[32,32,128]{2,1,0:T(8,128)(2,1)S(1)} collective-permute-done((bf16[32,32,128]{2,1,0:T(8,128)(2,1)S(1)}, bf16[32,32,128]{2,1,0:T(8,128)(2,1)S(1)}, u32[]{:S(2)}, u32[]{:S(2)}) %collective-permute-start.5) | collective-permute-done | bytes 262176 | tf_op jit(solution)/shard_map/ppermute | solution.py:373
  29.8 3.7 %collective-permute-done.9.rest_10_ = bf16[32,32,128]{2,1,0:T(8,128)(2,1)S(1)} collective-permute-done((bf16[32,32,128]{2,1,0:T(8,128)(2,1)S(1)}, bf16[32,32,128]{2,1,0:T(8,128)(2,1)S(1)}, u32[]{:S(2)}, u32[]{:S(2)}) %collective-permute-start.9) | collective-permute-done | bytes 262176 | tf_op jit(solution)/shard_map/ppermute | solution.py:373
  33.5 40.0 %turn.1.rest_12_ = bf16[1024,64,128]{2,1,0:T(8,128)(2,1)} custom-call(bf16[64,64,1024]{2,1,0:T(8,128)(2,1)} %bitcast.23), custom_call_target="tpu_custom_call" | custom-call | flops 2147483648 | bytes 24000000 | tf_op jit(solution)/shard_map/turn/pallas_call | solution.py:118
  75.9 27.5 %tasks.1 = (f32[32,32,128]{2,1,0:T(8,128)}, bf16[96,32,128]{2,1,0:T(8,128)(2,1)}) custom-call(s32[1]{0:T(128)} %bitcast.1.live_ref, s32[1024]{0:T(1024)} %get-tuple-element.13.source_ref, s32[1024]{0:T(1024)} %get-tuple-element.11.target_ref, bf16[32,32,128]{2,1,0:T(8,128)(2,1)} %coefs.1.rest_0_.coef_ref, bf16[32,32,128]{2,1,0:T(8,128)(2,1)} %copy-done, ...), custom_call_target="tpu_custom_call" | custom-call | flops 4294967296 | bytes 24000000 | tf_op jit(solution)/shard_map/tasks/pallas_call | solution.py:203
  106.0 1.9 %concatenate.25 = bf16[126,4096]{1,0:T(8,128)(2,1)S(1)} concatenate(bf16[64,4096]{1,0:T(8,128)(2,1)S(1)} %dynamic-slice_bitcast_fusion, bf16[32,4096]{1,0:T(8,128)(2,1)S(1)} %dynamic-slice_bitcast_fusion.1, bf16[16,4096]{1,0:T(8,128)(2,1)S(1)} %dynamic-slice_bitcast_fusion.2, bf16[8,4096]{1,0:T(8,128)(2,1)} %dynamic-slice_bitcast_fusion.3, ...), dimensions={0} | concatenate | bytes 2064384 | tf_op jit(solution)/shard_map/concatenate | solution.py:441
  108.0 3.5 %reshape.31.mats_ref = bf16[63,128,64]{2,1,0:T(8,128)(2,1)} reshape(bf16[126,4096]{1,0:T(8,128)(2,1)S(1)} %concatenate.25) | data formatting | bytes 2064384 | tf_op jit(solution)/shard_map/reshape | solution.py:441
  111.4 3.6 %up.1 = f32[32,64]{1,0:T(8,128)} custom-call(bf16[32,32,128]{2,1,0:T(8,128)(2,1)} %coefs.1.rest_0_.coef_ref, bf16[63,128,64]{2,1,0:T(8,128)(2,1)} %reshape.31.mats_ref), custom_call_target="tpu_custom_call" | custom-call | flops 264241152 | bytes 1032192 | tf_op jit(solution)/shard_map/up/pallas_call | solution.py:231
  115.1 1.4 collective-permute-done.13
  117.2 12.4 %collective-permute-start.14 = (f32[2,32,64]{2,1,0:T(8,128)S(1)}, f32[2,32,64]{2,1,0:T(8,128)S(1)}, u32[]{:S(2)}, u32[]{:S(2)}) collective-permute-start(f32[2,32,64]{2,1,0:T(8,128)S(1)} %pad_maximum_fusion.4), channel_id=1, source_target_pairs={{0,2},{1,3},{2,0},{3,1},{4,6},{5,7},{6,4},{7,5},{8,10},{9,11},{10,... | collective-permute-start | bytes 49160 | tf_op jit(solution)/shard_map/ppermute | solution.py:373
  132.8 1.8 %root.1 = f32[32,64]{1,0:T(8,128)} custom-call(f32[4,32,64]{2,1,0:T(8,128)} %pad_maximum_fusion.2.nodes_ref, bf16[6,64,64]{2,1,0:T(8,128)(2,1)} %reshape.32.mats_ref.crown_ref, s32[1]{0:T(128)} %bitcast.13.helper_ref), custom_call_target="tpu_custom_call" | custom-call | flops 12582912 | bytes 49152 | tf_op jit(solution)/shard_map/root/pallas_call | solution.py:258
  135.9 2.7 %collective-permute-done.15 = f32[1,32,64]{2,1,0:T(8,128)S(1)} collective-permute-done((f32[1,32,64]{2,1,0:T(8,128)}, f32[1,32,64]{2,1,0:T(8,128)S(1)}, u32[]{:S(2)}, u32[]{:S(2)}) %collective-permute-start.15) | collective-permute-done | bytes 8224 | tf_op jit(solution)/shard_map/ppermute | solution.py:373
  139.3 3.1 %collective-permute-start.16 = (f32[2,32,64]{2,1,0:T(8,128)S(1)}, f32[2,32,64]{2,1,0:T(8,128)S(1)}, u32[]{:S(2)}, u32[]{:S(2)}) collective-permute-start(f32[2,32,64]{2,1,0:T(8,128)S(1)} %pad_maximum_fusion.5), channel_id=1, source_target_pairs={{0,8},{4,12},{8,0},{12,4},{16,24},{20,28},{24,16},{28,20},{1,9},{5... | collective-permute-start | bytes 49160 | tf_op jit(solution)/shard_map/ppermute | solution.py:373
  145.0 3.0 %collective-permute-start.17 = (f32[4,32,64]{2,1,0:T(8,128)S(1)}, f32[4,32,64]{2,1,0:T(8,128)S(1)}, u32[]{:S(2)}, u32[]{:S(2)}) collective-permute-start(f32[4,32,64]{2,1,0:T(8,128)S(1)} %pad_maximum_fusion.3), channel_id=1, source_target_pairs={{0,16},{4,20},{8,24},{12,28},{16,0},{20,4},{24,8},{28,12},{1,17},{... | collective-permute-start | bytes 98312 | tf_op jit(solution)/shard_map/ppermute | solution.py:373
  150.5 4.5 %near.1.rest_4_ = f32[32,8192]{1,0:T(8,128)} custom-call(bf16[32,8192]{1,0:T(8,128)(2,1)} %x_ref.3, bf16[64,128,128]{2,1,0:T(8,128)(2,1)} %near_ref.1), custom_call_target="tpu_custom_call" | custom-call | flops 67108864 | bytes 4000000 | tf_op jit(solution)/shard_map/near/pallas_call | solution.py:84
  155.7 5.4 %down.1.rest_2_ = f32[32,32,128]{2,1,0:T(8,128)} custom-call(f32[8,32,64]{2,1,0:T(8,128)} %pad_maximum_fusion.1.roots_ref, bf16[14,64,64]{2,1,0:T(8,128)(2,1)} %reshape.34.top_ref, bf16[14,64,64]{2,1,0:T(8,128)(2,1)} %reshape.35.link_ref, bf16[6,64,64]{2,1,0:T(8,128)(2,1)} %reshape.32.mats_ref.crown_ref, bf16[63,128,64]{2,1,0:T(8,128)(2,1)} %reshape.31.mats_ref, ...), custom_call_target="tpu_custom_call" | custom-call | flops 264241152 | bytes 1032192 | tf_op jit(solution)/shard_map/down/pallas_call | solution.py:320
  162.5 4.2 %final.1 = bf16[32,8192]{1,0:T(8,128)(2,1)} custom-call(f32[32,32,128]{2,1,0:T(8,128)} %get-tuple-element.7.own_ref, bf16[32,32,128]{2,1,0:T(8,128)(2,1)} %slice.25.rest_0_, bf16[32,32,128]{2,1,0:T(8,128)(2,1)} %copy-done.10, f32[32,32,128]{2,1,0:T(8,128)} %down.1.rest_2_, bf16[32,128,128]{2,1,0:T(8,128)(2,1)} %bitcast.25, f32[32,8192]{1,0:T(8,128)} %near.1.rest_4_), custom_call_target="tpu_custom_call" | custom-call | flops 67108864 | bytes 5000000 | tf_op jit(solution)/shard_map/final/pallas_call | solution.py:359
  (76 shorter events, 23.3 us)
Async XLA Ops:
  3.9 22.8 %collective-permute-start = (bf16[32,32,128]{2,1,0:T(8,128)(2,1)}, bf16[32,32,128]{2,1,0:T(8,128)(2,1)S(1)}, u32[]{:S(2)}, u32[]{:S(2)}) collective-permute-start(bf16[32,32,128]{2,1,0:T(8,128)(2,1)} %coefs.1.rest_0_.coef_ref), channel_id=1, source_target_pairs={{0,1},{1,0},{2,3},{3,2},{4,5},{5,4},{6,7},{7,6},{8,9},{9,8},{10,11... | collective-permute-start | bytes 786440 | tf_op jit(solution)/shard_map/ppermute | solution.py:373
  4.4 21.8 %collective-permute-start.1 = (bf16[32,32,128]{2,1,0:T(8,128)(2,1)}, bf16[32,32,128]{2,1,0:T(8,128)(2,1)S(1)}, u32[]{:S(2)}, u32[]{:S(2)}) collective-permute-start(bf16[32,32,128]{2,1,0:T(8,128)(2,1)} %coefs.1.rest_0_.coef_ref), channel_id=1, source_target_pairs={{0,2},{1,3},{2,0},{3,1},{4,6},{5,7},{6,4},{7,5},{8,10},{9,11},{10,... | collective-permute-start | bytes 786440 | tf_op jit(solution)/shard_map/ppermute | solution.py:373
  6.9 8.6 %collective-permute-start.3 = (bf16[32,32,128]{2,1,0:T(8,128)(2,1)}, bf16[32,32,128]{2,1,0:T(8,128)(2,1)S(1)}, u32[]{:S(2)}, u32[]{:S(2)}) collective-permute-start(bf16[32,32,128]{2,1,0:T(8,128)(2,1)} %coefs.1.rest_0_.coef_ref), channel_id=1, source_target_pairs={{0,4},{4,0},{8,12},{12,8},{16,20},{20,16},{24,28},{28,24},{1,5},{5... | collective-permute-start | bytes 786440 | tf_op jit(solution)/shard_map/ppermute | solution.py:373
  15.5 58.0 %copy-start.2 = (bf16[32,32,128]{2,1,0:T(8,128)(2,1)}, bf16[32,32,128]{2,1,0:T(8,128)(2,1)S(1)}, u32[]{:S(2)}) copy-start(bf16[32,32,128]{2,1,0:T(8,128)(2,1)S(1)} %collective-permute-done.3.rest_4_) | copy-start | bytes 786436
  15.5 8.6 %collective-permute-start.7 = (bf16[32,32,128]{2,1,0:T(8,128)(2,1)S(1)}, bf16[32,32,128]{2,1,0:T(8,128)(2,1)S(1)}, u32[]{:S(2)}, u32[]{:S(2)}) collective-permute-start(bf16[32,32,128]{2,1,0:T(8,128)(2,1)S(1)} %collective-permute-done.3.rest_4_), channel_id=1, source_target_pairs={{0,8},{8,16},{16,24},{12,4},{20,12},{28,20},{1,9},{9,17},{17,25},{... | collective-permute-start | bytes 786440 | tf_op jit(solution)/shard_map/ppermute | solution.py:400
  20.6 9.2 %collective-permute-start.5 = (bf16[32,32,128]{2,1,0:T(8,128)(2,1)S(1)}, bf16[32,32,128]{2,1,0:T(8,128)(2,1)S(1)}, u32[]{:S(2)}, u32[]{:S(2)}) collective-permute-start(bf16[32,32,128]{2,1,0:T(8,128)(2,1)S(1)} %collective-permute-done.3.rest_4_), channel_id=1, source_target_pairs={{0,2},{1,3},{2,0},{3,1},{4,6},{5,7},{6,4},{7,5},{8,10},{9,11},{10,... | collective-permute-start | bytes 786440 | tf_op jit(solution)/shard_map/ppermute | solution.py:373
  24.1 49.5 %copy-start.3 = (bf16[32,32,128]{2,1,0:T(8,128)(2,1)}, bf16[32,32,128]{2,1,0:T(8,128)(2,1)S(1)}, u32[]{:S(2)}) copy-start(bf16[32,32,128]{2,1,0:T(8,128)(2,1)S(1)} %collective-permute-done.7.rest_8_) | copy-start | bytes 786436
  24.1 9.4 %collective-permute-start.9 = (bf16[32,32,128]{2,1,0:T(8,128)(2,1)S(1)}, bf16[32,32,128]{2,1,0:T(8,128)(2,1)S(1)}, u32[]{:S(2)}, u32[]{:S(2)}) collective-permute-start(bf16[32,32,128]{2,1,0:T(8,128)(2,1)S(1)} %collective-permute-done.7.rest_8_), channel_id=1, source_target_pairs={{0,2},{1,3},{2,0},{3,1},{4,6},{5,7},{6,4},{7,5},{8,10},{9,11},{10,... | collective-permute-start | bytes 786440 | tf_op jit(solution)/shard_map/ppermute | solution.py:373
  26.2 48.8 %collective-permute-start.4 = (bf16[32,32,128]{2,1,0:T(8,128)(2,1)S(1)}, bf16[32,32,128]{2,1,0:T(8,128)(2,1)S(1)}, u32[]{:S(2)}, u32[]{:S(2)}) collective-permute-start(bf16[32,32,128]{2,1,0:T(8,128)(2,1)S(1)} %collective-permute-done.3.rest_4_), channel_id=1, source_target_pairs={{0,1},{1,0},{2,3},{3,2},{4,5},{5,4},{6,7},{7,6},{8,9},{9,8},{10,11... | collective-permute-start | bytes 786440 | tf_op jit(solution)/shard_map/ppermute | solution.py:373
  26.2 47.4 %copy-start.1 = (bf16[32,32,128]{2,1,0:T(8,128)(2,1)}, bf16[32,32,128]{2,1,0:T(8,128)(2,1)S(1)}, u32[]{:S(2)}) copy-start(bf16[32,32,128]{2,1,0:T(8,128)(2,1)S(1)} %collective-permute-done.1.rest_2_) | copy-start | bytes 786436
  26.2 48.7 %collective-permute-start.2 = (bf16[32,32,128]{2,1,0:T(8,128)(2,1)S(1)}, bf16[32,32,128]{2,1,0:T(8,128)(2,1)S(1)}, u32[]{:S(2)}, u32[]{:S(2)}) collective-permute-start(bf16[32,32,128]{2,1,0:T(8,128)(2,1)S(1)} %collective-permute-done.1.rest_2_), channel_id=1, source_target_pairs={{0,1},{1,0},{2,3},{3,2},{4,5},{5,4},{6,7},{7,6},{8,9},{9,8},{10,11... | collective-permute-start | bytes 786440 | tf_op jit(solution)/shard_map/ppermute | solution.py:373
  26.7 46.9 %copy-start = (bf16[32,32,128]{2,1,0:T(8,128)(2,1)}, bf16[32,32,128]{2,1,0:T(8,128)(2,1)S(1)}, u32[]{:S(2)}) copy-start(bf16[32,32,128]{2,1,0:T(8,128)(2,1)S(1)} %collective-permute-done.rest_1_) | copy-start | bytes 786436
  26.7 48.3 %collective-permute-start.8 = (bf16[32,32,128]{2,1,0:T(8,128)(2,1)S(1)}, bf16[32,32,128]{2,1,0:T(8,128)(2,1)S(1)}, u32[]{:S(2)}, u32[]{:S(2)}) collective-permute-start(bf16[32,32,128]{2,1,0:T(8,128)(2,1)S(1)} %collective-permute-done.7.rest_8_), channel_id=1, source_target_pairs={{0,1},{1,0},{2,3},{3,2},{4,5},{5,4},{6,7},{7,6},{8,9},{9,8},{10,11... | collective-permute-start | bytes 786440 | tf_op jit(solution)/shard_map/ppermute | solution.py:373
  29.8 43.8 %copy-start.4 = (bf16[32,32,128]{2,1,0:T(8,128)(2,1)}, bf16[32,32,128]{2,1,0:T(8,128)(2,1)S(1)}, u32[]{:S(2)}) copy-start(bf16[32,32,128]{2,1,0:T(8,128)(2,1)S(1)} %collective-permute-done.5.rest_6_) | copy-start | bytes 786436
  29.8 45.1 %collective-permute-start.6 = (bf16[32,32,128]{2,1,0:T(8,128)(2,1)S(1)}, bf16[32,32,128]{2,1,0:T(8,128)(2,1)S(1)}, u32[]{:S(2)}, u32[]{:S(2)}) collective-permute-start(bf16[32,32,128]{2,1,0:T(8,128)(2,1)S(1)} %collective-permute-done.5.rest_6_), channel_id=1, source_target_pairs={{0,1},{1,0},{2,3},{3,2},{4,5},{5,4},{6,7},{7,6},{8,9},{9,8},{10,11... | collective-permute-start | bytes 786440 | tf_op jit(solution)/shard_map/ppermute | solution.py:373
  33.5 41.4 %collective-permute-start.10 = (bf16[32,32,128]{2,1,0:T(8,128)(2,1)S(1)}, bf16[32,32,128]{2,1,0:T(8,128)(2,1)}, u32[]{:S(2)}, u32[]{:S(2)}) collective-permute-start(bf16[32,32,128]{2,1,0:T(8,128)(2,1)S(1)} %collective-permute-done.9.rest_10_), channel_id=1, source_target_pairs={{0,1},{1,0},{2,3},{3,2},{4,5},{5,4},{6,7},{7,6},{8,9},{9,8},{10,11... | collective-permute-start | bytes 786440 | tf_op jit(solution)/shard_map/ppermute | solution.py:373
  104.5 37.9 %collective-permute-start.11 = (bf16[64,32,128]{2,1,0:T(8,128)(2,1)S(1)}, bf16[64,32,128]{2,1,0:T(8,128)(2,1)S(1)}, u32[]{:S(2)}, u32[]{:S(2)}) collective-permute-start(bf16[64,32,128]{2,1,0:T(8,128)(2,1)S(1)} %pad_maximum_fusion), channel_id=1, source_target_pairs={{0,1},{1,0},{2,3},{3,2},{4,5},{5,4},{6,7},{7,6},{8,9},{9,8},{10,11... | collective-permute-start | bytes 1572872 | tf_op jit(solution)/shard_map/ppermute | solution.py:373
  106.0 42.7 %copy-start.12 = (bf16[14,4096]{1,0:T(8,128)(2,1)S(1)}, bf16[14,4096]{1,0:T(8,128)(2,1)}, u32[]{:S(2)}) copy-start(bf16[14,4096]{1,0:T(8,128)(2,1)} %param.13) | copy-start | bytes 344068
  115.1 1.4 collective-permute-start.13
  117.2 14.3 %collective-permute-start.14 = (f32[2,32,64]{2,1,0:T(8,128)S(1)}, f32[2,32,64]{2,1,0:T(8,128)S(1)}, u32[]{:S(2)}, u32[]{:S(2)}) collective-permute-start(f32[2,32,64]{2,1,0:T(8,128)S(1)} %pad_maximum_fusion.4), channel_id=1, source_target_pairs={{0,2},{1,3},{2,0},{3,1},{4,6},{5,7},{6,4},{7,5},{8,10},{9,11},{10,... | collective-permute-start | bytes 49160 | tf_op jit(solution)/shard_map/ppermute | solution.py:373
  134.7 3.9 %collective-permute-start.15 = (f32[1,32,64]{2,1,0:T(8,128)}, f32[1,32,64]{2,1,0:T(8,128)S(1)}, u32[]{:S(2)}, u32[]{:S(2)}) collective-permute-start(f32[1,32,64]{2,1,0:T(8,128)} %bitcast.26), channel_id=1, source_target_pairs={{0,4},{4,0},{8,12},{12,8},{16,20},{20,16},{24,28},{28,24},{1,5},{5... | collective-permute-start | bytes 24584 | tf_op jit(solution)/shard_map/ppermute | solution.py:373
  139.3 5.0 %collective-permute-start.16 = (f32[2,32,64]{2,1,0:T(8,128)S(1)}, f32[2,32,64]{2,1,0:T(8,128)S(1)}, u32[]{:S(2)}, u32[]{:S(2)}) collective-permute-start(f32[2,32,64]{2,1,0:T(8,128)S(1)} %pad_maximum_fusion.5), channel_id=1, source_target_pairs={{0,8},{4,12},{8,0},{12,4},{16,24},{20,28},{24,16},{28,20},{1,9},{5... | collective-permute-start | bytes 49160 | tf_op jit(solution)/shard_map/ppermute | solution.py:373
  143.4 18.4 %collective-permute-start.12 = (bf16[32,32,128]{2,1,0:T(8,128)(2,1)S(1)}, bf16[32,32,128]{2,1,0:T(8,128)(2,1)S(1)}, u32[]{:S(2)}, u32[]{:S(2)}) collective-permute-start(bf16[32,32,128]{2,1,0:T(8,128)(2,1)S(1)} %add_convert_fusion), channel_id=1, source_target_pairs={{0,2},{1,3},{2,0},{3,1},{4,6},{5,7},{6,4},{7,5},{8,10},{9,11},{10,... | collective-permute-start | bytes 786440 | tf_op jit(solution)/shard_map/ppermute | solution.py:373
  145.0 10.0 %collective-permute-start.17 = (f32[4,32,64]{2,1,0:T(8,128)S(1)}, f32[4,32,64]{2,1,0:T(8,128)S(1)}, u32[]{:S(2)}, u32[]{:S(2)}) collective-permute-start(f32[4,32,64]{2,1,0:T(8,128)S(1)} %pad_maximum_fusion.3), channel_id=1, source_target_pairs={{0,16},{4,20},{8,24},{12,28},{16,0},{20,4},{24,8},{28,12},{1,17},{... | collective-permute-start | bytes 98312 | tf_op jit(solution)/shard_map/ppermute | solution.py:373
  (11 other events, 211.4 us)

commit v2 on v1

v2 whole, which is shorter than its diff:
```python
import functools

import jax
import jax.numpy as jnp
from jax import lax
from jax.experimental import pallas as pl
from jax.experimental.pallas import tpu as pltpu
from jax.sharding import PartitionSpec as P

BF = jnp.bfloat16
F32 = jnp.float32
NT = (((1,), (1,)), ((), ()))
NN = (((1,), (0,)), ((), ()))
BLOCK = 128
STEP = 16


def dot(a, b, dims=NN):
    return lax.dot_general(a, b, dims, preferred_element_type=F32)


def cost(flops, size):
    return pl.CostEstimate(flops=flops, bytes_accessed=size, transcendentals=0)


def limit(mebibytes):
    return pltpu.CompilerParams(vmem_limit_bytes=mebibytes << 20)


def lane_low(shape, width):
    return lax.broadcasted_iota(jnp.int32, shape, 1) < width


def split_rows(value):
    high = value.astype(BF)
    low = (value - high.astype(F32)).astype(BF)
    return jnp.concatenate([high, low], axis=0)


def precise(value, matrix, dims=NN):
    rows = value.shape[0]
    both = dot(split_rows(value), matrix, dims)
    return both[:rows] + both[rows:]


def coef_kernel(x_ref, basis_ref, out_ref):
    pairs, rhs, wide = out_ref.shape
    leaf = basis_ref.shape[-1]
    low = lane_low((rhs, wide), wide // 2)
    for p in range(pairs):
        first = x_ref[:, 2 * p * leaf : (2 * p + 1) * leaf]
        second = x_ref[:, (2 * p + 1) * leaf : (2 * p + 2) * leaf]
        both = dot(jnp.concatenate([first, second], axis=0), basis_ref[p], NT)
        out_ref[p] = jnp.where(low, both[:rhs], both[rhs:]).astype(BF)


def leaf_coefs(charges, basis_pairs):
    rhs = charges.shape[0]
    pairs, wide, leaf = basis_pairs.shape
    steps = 4
    per = pairs // steps
    return pl.pallas_call(
        coef_kernel,
        grid=(steps,),
        out_shape=jax.ShapeDtypeStruct((pairs, rhs, wide), BF),
        in_specs=[
            pl.BlockSpec((rhs, per * 2 * leaf), lambda b: (0, b)),
            pl.BlockSpec((per, wide, leaf), lambda b: (b, 0, 0)),
        ],
        out_specs=pl.BlockSpec((per, rhs, wide), lambda b: (b, 0, 0)),
        cost_estimate=cost(pairs * 2 * rhs * wide * leaf * 2, 2_000_000),
        compiler_params=limit(8),
        name="coefs",
    )(charges, basis_pairs)


def near_kernel(x_ref, near_ref, out_ref):
    leaf = near_ref.shape[-1]
    for k in range(near_ref.shape[0]):
        here = slice(k * leaf, (k + 1) * leaf)
        out_ref[:, here] = dot(x_ref[:, here], near_ref[k], NT)


def near_part(charges, near_field):
    rhs = charges.shape[0]
    leaves, leaf, _ = near_field.shape
    steps = 4
    per = leaves // steps
    return pl.pallas_call(
        near_kernel,
        grid=(steps,),
        out_shape=jax.ShapeDtypeStruct(charges.shape, F32),
        in_specs=[
            pl.BlockSpec((rhs, per * leaf), lambda b: (0, b)),
            pl.BlockSpec((per, leaf, leaf), lambda b: (b, 0, 0)),
        ],
        out_specs=pl.BlockSpec((rhs, per * leaf), lambda b: (0, b)),
        cost_estimate=cost(leaves * rhs * leaf * leaf * 2, 4_000_000),
        compiler_params=limit(8),
        name="near",
    )(charges, near_field)


def shuffle(size, blocks, back=False):
    wide = size * blocks
    row = lax.broadcasted_iota(jnp.int32, (wide, wide), 0)
    col = lax.broadcasted_iota(jnp.int32, (wide, wide), 1)
    if back:
        row, col = col, row
    inside = col % size
    source = 2 * (inside % (size // 2)) + inside // (size // 2) + col - inside
    return (row == source).astype(BF)


def turn_kernel(in_ref, out_ref, turned):
    rank = in_ref.shape[0]
    tasks = in_ref.shape[2]
    pitch = rank + 1
    row = lax.broadcasted_iota(jnp.int32, (tasks, tasks), 0)
    col = lax.broadcasted_iota(jnp.int32, (tasks, tasks), 1)
    unit = (row == col).astype(BF)

    @pl.loop(0, rank // 8)
    def _(step):
        for k in range(8):
            slab = in_ref[step * 8 + k]
            twice = jnp.concatenate([slab, slab], axis=0)
            place = step * 4 + k // 2 + (k % 2) * (rank // 2)
            turned[pl.ds(place, tasks, stride=pitch), :] = dot(unit, twice, NT)

    @pl.loop(0, tasks // 8)
    def _(step):
        base = pl.multiple_of(step * 8 * pitch, 8)
        for k in range(8):
            out_ref[step * 8 + k] = turned[pl.ds(base + k * pitch, rank), :].astype(BF)


def turn_blocks(blocks):
    rank, _, slots = blocks.shape
    wide = 2 * rank
    return pl.pallas_call(
        turn_kernel,
        grid=(slots // BLOCK,),
        out_shape=jax.ShapeDtypeStruct((slots, rank, wide), BF),
        in_specs=[pl.BlockSpec((rank, rank, BLOCK), lambda b: (0, 0, b))],
        out_specs=pl.BlockSpec((BLOCK, rank, wide), lambda b: (b, 0, 0)),
        scratch_shapes=[pltpu.VMEM((BLOCK * (rank + 1), wide), F32)],
        cost_estimate=cost(slots * rank * wide * 256, 24_000_000),
        compiler_params=limit(16),
        name="turn",
    )(blocks)


def task_kernel(parts, helpers, *refs):
    live_ref, source_ref, target_ref = refs[:3]
    window_refs = refs[3 : 3 + parts]
    blocks_ref, own_ref, send_ref, kept_ref, window, sums, more, ahead, later = refs[
        3 + parts :
    ]
    pairs, rhs, wide = window_refs[0].shape
    rank = wide // 2
    leaves = 2 * pairs * helpers
    low = lane_low((rhs, wide), rank)

    for k, ref in enumerate(window_refs):

        @pl.loop(0, pairs // 8)
        def _(step):
            for j in range(8):
                p = step * 8 + j
                pair = ref[p]
                none = jnp.zeros_like(pair)
                window[2 * (p + k * pairs)] = jnp.where(low, pair, none)
                window[2 * (p + k * pairs) + 1] = jnp.where(low, none, pair)

    @pl.loop(0, sums.shape[0] // 8)
    def _(step):
        for j in range(8):
            sums[step * 8 + j] = jnp.zeros(sums.shape[1:], F32)
            more[step * 8 + j] = jnp.zeros(sums.shape[1:], F32)

    later[...] = jnp.zeros_like(later)

    def product(slot):
        return dot(window[source_ref[slot]], blocks_ref[slot], NT)

    def add(buffer, first, valid):
        for k in range(STEP):
            place = target_ref[jnp.maximum(first, 0) + k]
            if valid is not None:
                place = jnp.where(valid, place, leaves)
            into = sums if k % 2 == 0 else more
            into[place] += buffer[k]

    count = (live_ref[0] + 2 * STEP - 1) // (2 * STEP)

    @pl.loop(0, count)
    def _(group):
        first = group * 2 * STEP
        for k in range(STEP):
            ahead[k] = product(first + k)
        add(later, first - STEP, group > 0)
        for k in range(STEP):
            later[k] = product(first + STEP + k)
        add(ahead, first, None)

    add(later, count * 2 * STEP - STEP, count > 0)

    def joined(p):
        return jnp.concatenate(
            [sums[2 * p] + more[2 * p], sums[2 * p + 1] + more[2 * p + 1]], axis=1
        )

    sent = kept = 0
    for block in range(helpers):
        if block == 0:
            ref, start = own_ref, 0
        elif block % 2:
            ref, start, sent = send_ref, sent * pairs, sent + 1
        else:
            ref, start, kept = kept_ref, kept * pairs, kept + 1

        @pl.loop(0, pairs // 8)
        def _(step):
            for j in range(8):
                p = step * 8 + j
                ref[start + p] = joined(block * pairs + p).astype(ref.dtype)


def couple(windows, turned, live, sources, targets, helpers):
    parts = len(windows)
    pairs, rhs, wide = windows[0].shape
    slots, rank, _ = turned.shape
    vmem = pl.BlockSpec(memory_space=pltpu.VMEM)
    smem = pl.BlockSpec(memory_space=pltpu.SMEM)
    shape = lambda blocks, kind: jax.ShapeDtypeStruct((blocks * pairs, rhs, wide), kind)
    acc = pltpu.VMEM((2 * pairs * helpers + 8, rhs, rank), F32)
    held = pltpu.VMEM((STEP, rhs, rank), F32)
    return pl.pallas_call(
        functools.partial(task_kernel, parts, helpers),
        in_specs=[smem] * 3 + [vmem] * (parts + 1),
        out_shape=[
            shape(1, F32),
            shape(helpers // 2, BF),
            shape(max(helpers // 2 - 1, 1), F32),
        ],
        scratch_shapes=[
            pltpu.VMEM((2 * parts * pairs, rhs, wide), BF),
            acc,
            acc,
            held,
            held,
        ],
        cost_estimate=cost(slots * rhs * rank * wide * 16, 24_000_000),
        compiler_params=limit(24),
        name="tasks",
    )(live, sources, targets, *windows, turned)


def level_plan(group_leaves, helpers):
    offset, count, big = 0, group_leaves, []
    while count // helpers >= 8:
        big.append((offset, count // helpers))
        offset += count
        count //= 2
    return big, offset, count


def up_kernel(plan, helper_ref, coef_ref, *refs):
    big, tail_offset, tail_count = plan
    level_refs = refs[: len(big)]
    tail_ref, top_ref, link_ref = refs[len(big) : len(big) + 3]
    node_ref, mats_ref, rest_ref, upper_ref, across_ref, scratch = refs[len(big) + 3 :]
    pairs, rhs, wide = coef_ref.shape
    rank = wide // 2
    helper = helper_ref[0]
    row = lax.broadcasted_iota(jnp.int32, (wide, rank), 0)
    col = lax.broadcasted_iota(jnp.int32, (wide, rank), 1)
    source = 2 * (col % (rank // 2)) + col // (rank // 2)
    first = (row == source).astype(BF)
    second = (row == source + rank).astype(BF)
    tiles = rank // 2
    pitch = tiles + 1

    def expand(rows, into, place, count):
        for s in range(tiles):
            piece = rows[:, wide * s : wide * (s + 1)].astype(F32)
            scratch[pl.ds(s, count, stride=pitch), :] = piece
        flat = jnp.concatenate(
            [scratch[n * pitch : n * pitch + tiles].astype(BF) for n in range(count)], axis=0
        )
        for half, matrix in enumerate((first, second)):
            turned = dot(flat, matrix).astype(BF)
            for n in range(count):
                into[place + n, half * tiles : (half + 1) * tiles] = turned[
                    n * tiles : (n + 1) * tiles
                ]

    def expand_all(ref, into, base, total):
        full = total // 16

        if full > 1:

            @pl.loop(0, full)
            def _(step):
                start = pl.multiple_of(step * 16, 16)
                expand(ref[pl.ds(start, 16), :], into, base + start, 16)

        elif full:
            expand(ref[0:16, :], into, base, 16)
        left = total - 16 * full
        if left:
            expand(ref[16 * full : total, :], into, base + 16 * full, left)

    base = 0
    for ref, (_, wanted) in zip(level_refs, big):
        expand_all(ref, mats_ref, base, wanted)
        base += wanted
    expand_all(tail_ref, rest_ref, 0, rest_ref.shape[0])
    expand_all(top_ref, upper_ref, 0, upper_ref.shape[0])
    expand_all(link_ref, across_ref, 0, across_ref.shape[0])

    coefs = dot(coef_ref[...].reshape(pairs * rhs, wide), shuffle(rank, 2)).astype(BF)
    nodes = [
        dot(coefs[p * rhs : (p + 1) * rhs], mats_ref[2 * p : 2 * p + 2].reshape(wide, rank))
        for p in range(pairs)
    ]
    base = 2 * pairs
    for _, wanted in big[1:]:
        joined = [jnp.concatenate(nodes[k : k + 2], axis=1) for k in range(0, wanted, 2)]
        nodes = [
            precise(j, mats_ref[base + 2 * p : base + 2 * p + 2].reshape(wide, rank))
            for p, j in enumerate(joined)
        ]
        base += wanted
    base = 0
    while len(nodes) > 1:
        wanted = len(nodes)
        joined = [jnp.concatenate(nodes[k : k + 2], axis=1) for k in range(0, wanted, 2)]
        start = base + helper * wanted
        nodes = [
            precise(j, rest_ref[pl.ds(start + 2 * p, 2)].reshape(wide, rank))
            for p, j in enumerate(joined)
        ]
        base += tail_count
        tail_count //= 2
    node_ref[0] = nodes[0]


def tree_up(coefs, rows, top, links, helper, helpers):
    pairs, rhs, wide = coefs.shape
    rank = wide // 2
    total, flat = rows.shape
    plan = level_plan((total + 2) // 2, helpers)
    big, tail_offset, tail_count = plan
    level_spec = lambda offset, wanted: pl.BlockSpec(
        (wanted, flat), lambda b, ref, o=offset // wanted: (o + ref[0], 0)
    )
    whole = lambda shape: pl.BlockSpec(shape, lambda b, ref: (0,) * len(shape))
    near = sum(wanted for _, wanted in big)
    outs = [
        jax.ShapeDtypeStruct((1, rhs, rank), F32),
        jax.ShapeDtypeStruct((near, rank, rank), BF),
        jax.ShapeDtypeStruct((total - tail_offset, rank, rank), BF),
        jax.ShapeDtypeStruct((top.shape[0], rank, rank), BF),
        jax.ShapeDtypeStruct((top.shape[0], rank, rank), BF),
    ]
    return pl.pallas_call(
        functools.partial(up_kernel, plan),
        grid_spec=pltpu.PrefetchScalarGridSpec(
            num_scalar_prefetch=1,
            grid=(1,),
            in_specs=[whole(coefs.shape)]
            + [level_spec(*level) for level in big]
            + [
                pl.BlockSpec(
                    (2 * tail_count, flat),
                    lambda b, ref, o=tail_offset // (2 * tail_count): (o, 0),
                ),
                whole(top.shape),
                whole(links.shape),
            ],
            out_specs=[whole(out.shape) for out in outs],
            scratch_shapes=[pltpu.VMEM((16 * (rank // 2 + 1), wide), F32)],
        ),
        out_shape=outs,
        cost_estimate=cost(1_500_000_000, 6_000_000),
        compiler_params=limit(20),
        name="up",
    )(helper, coefs, *[rows] * (len(big) + 1), top, links)


def listed(refs):
    return [ref[k] for ref in refs for k in range(ref.shape[0])]


def root_kernel(count, start, helper_ref, *refs):
    mats_ref, root_ref = refs[count:]
    helper = helper_ref[0]
    nodes = listed(refs[:count])
    offset = start
    level = 0
    while len(nodes) > 1:
        home = lax.shift_right_logical(helper, level)
        lifted = [
            precise(node, mats_ref[offset + jnp.bitwise_xor(home, k)])
            for k, node in enumerate(nodes)
        ]
        offset += len(nodes)
        level += 1
        nodes = [lifted[2 * k] + lifted[2 * k + 1] for k in range(len(nodes) // 2)]
    root_ref[0] = nodes[0]


def group_root(nodes, mats, helper, helpers):
    vmem = pl.BlockSpec(memory_space=pltpu.VMEM)
    start = mats.shape[0] - (2 * helpers - 2)
    return pl.pallas_call(
        functools.partial(root_kernel, len(nodes), start),
        out_shape=jax.ShapeDtypeStruct((1, *nodes[0].shape[1:]), F32),
        in_specs=[pl.BlockSpec(memory_space=pltpu.SMEM)] + [vmem] * (len(nodes) + 1),
        cost_estimate=cost(50_000_000, 300_000),
        compiler_params=limit(8),
        name="root",
    )(helper, *nodes, mats)


def down_kernel(count, plan, helpers, place_ref, *refs):
    big, _, tail_count = plan
    top_ref, link_ref, rest_ref, mats_ref, out_ref = refs[count:]
    group, helper = place_ref[0], place_ref[1]
    nodes = listed(refs[:count])
    offset = 0
    level = 0
    far = []
    moves = []
    while len(nodes) > 1:
        home = lax.shift_right_logical(group, level)
        far.append(precise(nodes[1], link_ref[offset + home], NT))
        moves.append(offset + home)
        if len(nodes) > 2:
            lifted = [
                precise(node, top_ref[offset + jnp.bitwise_xor(home, k)])
                for k, node in enumerate(nodes)
            ]
        else:
            lifted = []
        offset += len(nodes)
        level += 1
        nodes = [lifted[2 * k] + lifted[2 * k + 1] for k in range(len(lifted) // 2)]
    down = far[-1]
    for t in range(len(far) - 2, -1, -1):
        down = far[t] + precise(down, top_ref[moves[t]], NT)
    rank = down.shape[1]
    wide = 2 * rank
    offset = rest_ref.shape[0]
    length = 2
    while length <= helpers:
        offset -= length
        home = helper // (helpers // length)
        down = precise(down, rest_ref[offset + home], NT)
        length *= 2

    nodes = [down]

    def step(ref, start):
        joined = [
            precise(node, ref[pl.ds(start + 2 * p, 2)].reshape(wide, rank), NT)
            for p, node in enumerate(nodes)
        ]
        return joined

    def halves(joined):
        return [part for j in joined for part in (j[:, :rank], j[:, rank:])]

    while length <= tail_count:
        offset -= length
        wanted = length // helpers
        nodes = halves(step(rest_ref, offset + helper * wanted))
        length *= 2
    offset = mats_ref.shape[0]
    for _, wanted in reversed(big):
        offset -= wanted
        joined = step(mats_ref, offset)
        if offset:
            nodes = halves(joined)
    for p, value in enumerate(joined):
        out_ref[p] = value


def tree_down(roots, top, links, rest, mats, place, pairs, helpers, group_leaves):
    _, rhs, rank = roots[0].shape
    vmem = pl.BlockSpec(memory_space=pltpu.VMEM)
    plan = level_plan(group_leaves, helpers)
    return pl.pallas_call(
        functools.partial(down_kernel, len(roots), plan, helpers),
        out_shape=jax.ShapeDtypeStruct((pairs, rhs, 2 * rank), F32),
        in_specs=[pl.BlockSpec(memory_space=pltpu.SMEM)] + [vmem] * (len(roots) + 4),
        cost_estimate=cost(mats.size * rhs * 16, 4 * mats.size),
        compiler_params=limit(12),
        name="down",
    )(place, *roots, top, links, rest, mats)


def final_kernel(count, own_ref, *rest):
    added = rest[:count]
    down_ref, basis_ref, near_ref, out_ref = rest[count:]
    pairs, rhs, wide = own_ref.shape
    leaf = basis_ref.shape[-1]
    low = lane_low((rhs, wide), wide // 2)
    total = own_ref[...] + down_ref[...]
    for ref in added:
        total = total + ref[...].astype(F32)
    field = total.astype(BF).reshape(pairs * rhs, wide)
    field = dot(field, shuffle(wide // 2, 2, back=True)).astype(BF)
    for p in range(pairs):
        mine = field[p * rhs : (p + 1) * rhs]
        none = jnp.zeros_like(mine)
        lhs = jnp.concatenate(
            [jnp.where(low, mine, none), jnp.where(low, none, mine)], axis=0
        )
        far = dot(lhs, basis_ref[p])
        for half in range(2):
            here = slice((2 * p + half) * leaf, (2 * p + half + 1) * leaf)
            out_ref[:, here] = (
                far[half * rhs : (half + 1) * rhs] + near_ref[:, here]
            ).astype(BF)


def finish(own, added, down, basis_pairs, near):
    pairs, rhs, wide = own.shape
    leaf = basis_pairs.shape[-1]
    steps = 4
    per = pairs // steps
    pair_spec = pl.BlockSpec((per, rhs, wide), lambda b: (b, 0, 0))
    flat_spec = pl.BlockSpec((rhs, per * 2 * leaf), lambda b: (0, b))
    return pl.pallas_call(
        functools.partial(final_kernel, len(added)),
        grid=(steps,),
        out_shape=jax.ShapeDtypeStruct(near.shape, BF),
        in_specs=[pair_spec] * (2 + len(added))
        + [pl.BlockSpec((per, wide, leaf), lambda b: (b, 0, 0)), flat_spec],
        out_specs=flat_spec,
        cost_estimate=cost(pairs * rhs * wide * leaf * 4, 5_000_000),
        compiler_params=limit(12),
        name="final",
    )(own, *added, down, basis_pairs, near)


def xor_move(value, axis, mask):
    count = lax.axis_size(axis)
    return lax.ppermute(value, axis, [(i, i ^ mask) for i in range(count)])


def gather_nodes(node, axis):
    left = lax.axis_size(axis)
    pieces = [node]
    stride = 1
    while left > 1:
        radix = min(8, left)
        payload = pieces[0] if len(pieces) == 1 else jnp.concatenate(pieces, axis=0)
        pieces = [payload] + [xor_move(payload, axis, m * stride) for m in range(1, radix)]
        stride *= radix
        left //= radix
    return pieces


def shards(
    charges,
    leaf_basis,
    near_field,
    local_transfer,
    top_transfer,
    top_coupling,
    leaf_coupling,
    task_target,
    task_source,
):
    helpers = lax.axis_size("helper")
    groups = lax.axis_size("leaf")
    helper = lax.axis_index("helper")
    group = lax.axis_index("leaf")
    own_leaves, rank, leaf = leaf_basis.shape
    group_leaves = own_leaves * helpers
    own_pairs = own_leaves // 2
    bits = helpers.bit_length() - 1

    basis_pairs = leaf_basis.reshape(own_pairs, 2 * rank, leaf)
    own = leaf_coefs(charges, basis_pairs)

    partner = xor_move(own, "leaf", 1)
    beyond = lax.ppermute(
        partner,
        "leaf",
        [(i, i + 2) for i in range(0, groups - 2, 2)]
        + [(i, i - 2) for i in range(3, groups, 2)],
    )

    def spread(block):
        blocks = {0: block}
        for bit in reversed(range(bits)):
            for k in sorted(blocks):
                blocks[k | 1 << bit] = xor_move(blocks[k], "helper", 1 << bit)
        return [blocks[k] for k in range(helpers)]

    windows = spread(own) + spread(partner) + spread(beyond)

    def place_of(leaf_index):
        owner = jnp.bitwise_xor(leaf_index // own_leaves, helper)
        return owner * own_leaves + leaf_index % own_leaves

    targets, sources = task_target[0], task_source[0]
    is_live = targets < group_leaves
    live = jnp.sum(is_live.astype(jnp.int32)).reshape(1)
    side = sources // group_leaves
    near_side = jnp.where(group % 2 == 0, 2, 0)
    slot = jnp.where(side == 1, 0, jnp.where(side == near_side, 1, 2))
    source_place = slot * group_leaves + place_of(sources % group_leaves)
    target_place = jnp.where(is_live, place_of(targets), group_leaves)

    top_node, mats, rest, top, links = tree_up(
        own, local_transfer[0], top_transfer, top_coupling, helper.reshape(1), helpers
    )
    turned = turn_blocks(jnp.transpose(leaf_coupling[0], (1, 2, 0)))
    near = near_part(charges, near_field)
    root = group_root(gather_nodes(top_node, "helper"), rest, helper.reshape(1), helpers)
    down = tree_down(
        gather_nodes(root, "leaf"),
        top,
        links,
        rest,
        mats,
        jnp.stack([group, helper]),
        own_pairs,
        helpers,
        group_leaves,
    )

    sums, sent, kept = couple(windows, turned, live, source_place, target_place, helpers)
    added = []
    for bit in range(bits):
        got = xor_move(sent, "helper", 1 << bit)
        added.append(got)
        if bit + 1 < bits:
            total = kept + got[own_pairs:].astype(F32)
            count = total.shape[0] // own_pairs
            odd = [k for k in range(count) if k % 2 == 0]
            even = [k for k in range(count) if k % 2]
            take = lambda picks: jnp.concatenate(
                [total[k * own_pairs : (k + 1) * own_pairs] for k in picks], axis=0
            )
            sent = take(odd).astype(BF)
            kept = take(even) if even else None
    return finish(sums, added, down, basis_pairs, near)


def solution(mesh):
    return jax.shard_map(
        shards,
        mesh=mesh,
        in_specs=(
            P(None, ("leaf", "helper")),
            P(("leaf", "helper"), None, None),
            P(("leaf", "helper"), None, None),
            P("leaf", None, None),
            P(),
            P(),
            P("leaf", "helper", None, None),
            P("leaf", "helper"),
            P("leaf", "helper"),
        ),
        out_specs=P(None, ("leaf", "helper")),
        check_vma=False,
    )
```

time: 168 us -> 125 us (0.74)
  Pallas kernels: 90.9 us -> 45 us
  waiting for transfers between devices: 19.7 us -> 27.2 us
  other arithmetic: 7.18 us -> 0.77 us
  starting transfers between devices: 30.1 us -> 34 us
    pallas_call x4, Pallas kernels: 38.4 us -> 16.5 us  [the longest x1 9.61 us: couple(): pl.pallas_call(functools.partial(task_kernel, parts, helpers), in_specs=[...]
    pallas_call x1, Pallas kernels: 40 us -> 23.3 us  [turn_blocks(): pl.pallas_call(turn_kernel, grid=(slots // BLOCK,), out_shape=jax.ShapeDt...]
    unnamed x32 -> x26, local copies, waits for them, and re-layouts: 1.66 us -> 17.2 us
    ppermute x17 -> x22, waiting for transfers between devices: 16.7 us -> 24.6 us  [xor_move(): return lax.ppermute(value, axis, [(i, i ^ mask) for i in range(count)])]
    dynamic_slice x6 -> x0, local copies, waits for them, and re-layouts: 7.18 us -> none  [shards(): lax.dynamic_slice_in_dim(rows, offset + helper * wanted, wanted, 0)]
    reshape x4 -> x0, local copies, waits for them, and re-layouts: 6.04 us -> none  [the longest x1 3.45 us: shards(): jnp.concatenate(picked, axis=0).reshape(own_leaves - 1, 2 * rank, rank)]
    concatenate x6 -> x0, other arithmetic: 4.24 us -> none  [the longest x5 4.19 us: gather_nodes(): nodes = jnp.concatenate([nodes, xor_move(nodes, axis, bit)], axis=0)]
    ppermute x17 -> x22, starting transfers between devices: 26.6 us -> 30.3 us  [xor_move(): return lax.ppermute(value, axis, [(i, i ^ mask) for i in range(count)])]
  transfers between devices with their start and end apart: 18 -> 23, of which waited for: 8 -> 8; matrix products, arithmetic and copies ran while one was open for 14% -> 1% of each run, Pallas kernels for 33% -> 26%
where the time goes in v2:
time: 125 us; the launch traced here: 124 us
  Pallas kernels  45 us (36%)
  starting transfers between devices  34 us (27%)
  waiting for transfers between devices  27.2 us (22%)
  local copies, waits for them, and re-layouts  17.2 us (14%)
    ppermute x22, starting transfers between devices, xor_move(): return lax.ppermute(value, axis, [(i, i ^ mask) for i in range(count)])  30.3 us
    ppermute x22, waiting for transfers between devices, xor_move(): return lax.ppermute(value, axis, [(i, i ^ mask) for i in range(count)])  24.6 us
    pallas_call x1, Pallas kernels, turn_blocks(): pl.pallas_call(turn_kernel, grid=(slots // BLOCK,), out_shape=jax.ShapeDt...  23.3 us
    unnamed x26, local copies, waits for them, and re-layouts  17.2 us
    pallas_call x1, Pallas kernels, couple(): pl.pallas_call(functools.partial(task_kernel, parts, helpers), in_specs=[...  9.61 us
    ppermute x1, starting transfers between devices, shards(): lax.ppermute(partner, 'leaf', [(i, i + 2) for i in range(0, groups - 2, 2...  3.73 us
    pallas_call x1, Pallas kernels, tree_up(): pl.pallas_call(functools.partial(up_kernel, plan), grid_spec=pltpu.Prefet...  3.41 us
    pallas_call x1, Pallas kernels, tree_down(): pl.pallas_call(functools.partial(down_kernel, len(roots), plan, helpers),...  3.19 us
  transfers between devices with their start and end apart: 23, of which 8 were waited for; matrix products, arithmetic and copies ran while one was open for 1% of the time, Pallas kernels for 26%

profile of v2, /device:TPU:0, one launch (start us, length us, event | category | flops | bytes accessed | tf_op | source)
XLA Modules:
  0.0 124.4 jit_solution(2047970542874183183)
XLA Ops:
  3.5 3.0 %collective-permute-start.3 = (bf16[32,32,128]{2,1,0:T(8,128)(2,1)S(1)}, bf16[32,32,128]{2,1,0:T(8,128)(2,1)S(1)}, u32[]{:S(2)}, u32[]{:S(2)}) collective-permute-start(bf16[32,32,128]{2,1,0:T(8,128)(2,1)S(1)} %coefs.1.refs_3_.coef_ref), channel_id=1, source_target_pairs={{0,4},{4,0},{8,12},{12,8},{16,20},{20,16},{24,28},{28,24},{1,5},{5... | collective-permute-start | bytes 786440 | tf_op jit(solution)/shard_map/ppermute | solution.py:552
  6.5 6.3 %collective-permute-done.3.refs_7_ = bf16[32,32,128]{2,1,0:T(8,128)(2,1)S(1)} collective-permute-done((bf16[32,32,128]{2,1,0:T(8,128)(2,1)S(1)}, bf16[32,32,128]{2,1,0:T(8,128)(2,1)S(1)}, u32[]{:S(2)}, u32[]{:S(2)}) %collective-permute-start.3) | collective-permute-done | bytes 262176 | tf_op jit(solution)/shard_map/ppermute | solution.py:552
  12.8 3.7 %collective-permute-start.7 = (bf16[32,32,128]{2,1,0:T(8,128)(2,1)S(1)}, bf16[32,32,128]{2,1,0:T(8,128)(2,1)S(1)}, u32[]{:S(2)}, u32[]{:S(2)}) collective-permute-start(bf16[32,32,128]{2,1,0:T(8,128)(2,1)S(1)} %collective-permute-done.3.refs_7_), channel_id=1, source_target_pairs={{0,8},{8,16},{16,24},{12,4},{20,12},{28,20},{1,9},{9,17},{17,25},{... | collective-permute-start | bytes 786440 | tf_op jit(solution)/shard_map/ppermute | solution.py:592
  18.6 2.6 %collective-permute-done.7.refs_11_ = bf16[32,32,128]{2,1,0:T(8,128)(2,1)S(1)} collective-permute-done((bf16[32,32,128]{2,1,0:T(8,128)(2,1)S(1)}, bf16[32,32,128]{2,1,0:T(8,128)(2,1)S(1)}, u32[]{:S(2)}, u32[]{:S(2)}) %collective-permute-start.7) | collective-permute-done | bytes 262176 | tf_op jit(solution)/shard_map/ppermute | solution.py:592
  22.7 3.0 %collective-permute-done.1.refs_5_ = bf16[32,32,128]{2,1,0:T(8,128)(2,1)S(1)} collective-permute-done((bf16[32,32,128]{2,1,0:T(8,128)(2,1)S(1)}, bf16[32,32,128]{2,1,0:T(8,128)(2,1)S(1)}, u32[]{:S(2)}, u32[]{:S(2)}) %collective-permute-start.1) | collective-permute-done | bytes 262176 | tf_op jit(solution)/shard_map/ppermute | solution.py:552
  26.3 5.1 %collective-permute-done.5.refs_9_ = bf16[32,32,128]{2,1,0:T(8,128)(2,1)S(1)} collective-permute-done((bf16[32,32,128]{2,1,0:T(8,128)(2,1)S(1)}, bf16[32,32,128]{2,1,0:T(8,128)(2,1)S(1)}, u32[]{:S(2)}, u32[]{:S(2)}) %collective-permute-start.5) | collective-permute-done | bytes 262176 | tf_op jit(solution)/shard_map/ppermute | solution.py:552
  31.4 3.3 %collective-permute-done.9.refs_13_ = bf16[32,32,128]{2,1,0:T(8,128)(2,1)S(1)} collective-permute-done((bf16[32,32,128]{2,1,0:T(8,128)(2,1)S(1)}, bf16[32,32,128]{2,1,0:T(8,128)(2,1)S(1)}, u32[]{:S(2)}, u32[]{:S(2)}) %collective-permute-start.9) | collective-permute-done | bytes 262176 | tf_op jit(solution)/shard_map/ppermute | solution.py:552
  34.8 3.4 %copy-done.3 = bf16[1,1024,64,64]{1,3,2,0:T(8,128)(2,1)S(1)} copy-done((bf16[1,1024,64,64]{1,3,2,0:T(8,128)(2,1)S(1)}, bf16[1,1024,64,64]{1,3,2,0:T(8,128)(2,1)}, u32[]{:S(2)}) %copy-start.3) | copy-done | bytes 8388632
  38.1 23.3 %turn.1.refs_15_ = bf16[1024,64,128]{2,1,0:T(8,128)(2,1)S(1)} custom-call(bf16[64,64,1024]{2,1,0:T(8,128)(2,1)S(1)} %bitcast.15), custom_call_target="tpu_custom_call" | custom-call | flops 2147483648 | bytes 24000000 | tf_op jit(solution)/shard_map/turn/pallas_call | solution.py:141
  61.4 5.8 %copy-done.1 = bf16[1024,64,128]{2,1,0:T(8,128)(2,1)} copy-done((bf16[1024,64,128]{2,1,0:T(8,128)(2,1)}, bf16[1024,64,128]{2,1,0:T(8,128)(2,1)S(1)}, u32[]{:S(2)}) %copy-start.1) | copy-done | bytes 16777240
  67.8 5.8 %copy-done.2 = bf16[1024,64,128]{2,1,0:T(8,128)(2,1)S(1)} copy-done((bf16[1024,64,128]{2,1,0:T(8,128)(2,1)S(1)}, bf16[1024,64,128]{2,1,0:T(8,128)(2,1)}, u32[]{:S(2)}) %copy-start.2) | copy-done | bytes 16777240
  73.6 9.6 %tasks.1 = (f32[32,32,128]{2,1,0:T(8,128)S(1)}, bf16[64,32,128]{2,1,0:T(8,128)(2,1)S(1)}, f32[32,32,128]{2,1,0:T(8,128)S(1)}) custom-call(s32[1]{0:T(128)} %bitcast.1.refs_0_, s32[1024]{0:T(1024)S(1)} %get-tuple-element.23.refs_1_, s32[1024]{0:T(1024)S(1)} %get-tuple-element.21.refs_2_, bf16[32,32,128]{2,1,0:T(8,128)(2,1)S(1)} %coefs.1.refs_3_.coef_ref, ...), custom_call_target="tpu_custom_call" | custom-call | flops 4294967296 | bytes 24000000 | tf_op jit(solution)/shard_map/tasks/pallas_call | solution.py:239
  83.3 1.9 %collective-permute-done.11.rest_0_ = bf16[64,32,128]{2,1,0:T(8,128)(2,1)S(1)} collective-permute-done((bf16[64,32,128]{2,1,0:T(8,128)(2,1)S(1)}, bf16[64,32,128]{2,1,0:T(8,128)(2,1)S(1)}, u32[]{:S(2)}, u32[]{:S(2)}) %collective-permute-start.11) | collective-permute-done | bytes 524320 | tf_op jit(solution)/shard_map/ppermute | solution.py:552
  85.3 9.6 %collective-permute-start.12 = (bf16[32,32,128]{2,1,0:T(8,128)(2,1)S(1)}, bf16[32,32,128]{2,1,0:T(8,128)(2,1)S(1)}, u32[]{:S(2)}, u32[]{:S(2)}) collective-permute-start(bf16[32,32,128]{2,1,0:T(8,128)(2,1)S(1)} %add_convert_fusion), channel_id=1, source_target_pairs={{0,2},{1,3},{2,0},{3,1},{4,6},{5,7},{6,4},{7,5},{8,10},{9,11},{10,... | collective-permute-start | bytes 786440 | tf_op jit(solution)/shard_map/ppermute | solution.py:552
  94.9 3.4 %up.1 = (f32[1,32,64]{2,1,0:T(8,128)S(1)}, bf16[120,64,64]{2,1,0:T(8,128)(2,1)S(1)}, bf16[30,64,64]{2,1,0:T(8,128)(2,1)S(1)}, bf16[14,64,64]{2,1,0:T(8,128)(2,1)S(1)}, bf16[14,64,64]{2,1,0:T(8,128)(2,1)S(1)}) custom-call(s32[1]{0:T(128)} %bitcast.7.helper_ref, bf16[32,32,128]{2,1,0:T(8,128)(2,1)S(1)} %coefs.1.refs_3_.coef_ref, ...), custom_call_target="tpu_custom_call" | custom-call | flops 1500000000 | bytes 6000000 | tf_op jit(solution)/shard_map/up/pallas_call | solution.py:368
  98.5 1.7 %collective-permute-start.15 = (f32[1,32,64]{2,1,0:T(8,128)S(1)}, f32[1,32,64]{2,1,0:T(8,128)S(1)}, u32[]{:S(2)}, u32[]{:S(2)}) collective-permute-start(f32[1,32,64]{2,1,0:T(8,128)S(1)} %get-tuple-element.16.refs_0_), channel_id=1, source_target_pairs={{0,3},{1,2},{2,1},{3,0},{4,7},{5,6},{6,5},{7,4},{8,11},{9,10},{10,... | collective-permute-start | bytes 24584 | tf_op jit(solution)/shard_map/ppermute | solution.py:552
  100.2 1.9 %collective-permute-done.14.refs_2_ = f32[1,32,64]{2,1,0:T(8,128)S(1)} collective-permute-done((f32[1,32,64]{2,1,0:T(8,128)S(1)}, f32[1,32,64]{2,1,0:T(8,128)S(1)}, u32[]{:S(2)}, u32[]{:S(2)}) %collective-permute-start.14) | collective-permute-done | bytes 8224 | tf_op jit(solution)/shard_map/ppermute | solution.py:552
  102.4 1.9 %collective-permute-start.17 = (f32[1,32,64]{2,1,0:T(8,128)S(1)}, f32[1,32,64]{2,1,0:T(8,128)S(1)}, u32[]{:S(2)}, u32[]{:S(2)}) collective-permute-start(f32[1,32,64]{2,1,0:T(8,128)S(1)} %root.1.refs_0_), channel_id=1, source_target_pairs={{0,8},{4,12},{8,0},{12,4},{16,24},{20,28},{24,16},{28,20},{1,9},{5... | collective-permute-start | bytes 24584 | tf_op jit(solution)/shard_map/ppermute | solution.py:552
  105.9 3.0 %collective-permute-start.19 = (f32[1,32,64]{2,1,0:T(8,128)S(1)}, f32[1,32,64]{2,1,0:T(8,128)S(1)}, u32[]{:S(2)}, u32[]{:S(2)}) collective-permute-start(f32[1,32,64]{2,1,0:T(8,128)S(1)} %root.1.refs_0_), channel_id=1, source_target_pairs={{0,16},{4,20},{8,24},{12,28},{16,0},{20,4},{24,8},{28,12},{1,17},{... | collective-permute-start | bytes 24584 | tf_op jit(solution)/shard_map/ppermute | solution.py:552
  109.0 3.2 %collective-permute-start.21 = (f32[1,32,64]{2,1,0:T(8,128)S(1)}, f32[1,32,64]{2,1,0:T(8,128)S(1)}, u32[]{:S(2)}, u32[]{:S(2)}) collective-permute-start(f32[1,32,64]{2,1,0:T(8,128)S(1)} %root.1.refs_0_), channel_id=1, source_target_pairs={{0,24},{4,28},{8,16},{12,20},{16,8},{20,12},{24,0},{28,4},{1,25},{... | collective-permute-start | bytes 24584 | tf_op jit(solution)/shard_map/ppermute | solution.py:552
  112.3 1.7 %collective-permute-start.22 = (f32[1,32,64]{2,1,0:T(8,128)S(1)}, f32[1,32,64]{2,1,0:T(8,128)S(1)}, u32[]{:S(2)}, u32[]{:S(2)}) collective-permute-start(f32[1,32,64]{2,1,0:T(8,128)S(1)} %root.1.refs_0_), channel_id=1, source_target_pairs={{0,28},{4,24},{8,20},{12,16},{16,12},{20,8},{24,4},{28,0},{1,29},{... | collective-permute-start | bytes 24584 | tf_op jit(solution)/shard_map/ppermute | solution.py:552
  115.7 3.0 %collective-permute-done.22.refs_7_ = f32[1,32,64]{2,1,0:T(8,128)S(1)} collective-permute-done((f32[1,32,64]{2,1,0:T(8,128)S(1)}, f32[1,32,64]{2,1,0:T(8,128)S(1)}, u32[]{:S(2)}, u32[]{:S(2)}) %collective-permute-start.22) | collective-permute-done | bytes 8224 | tf_op jit(solution)/shard_map/ppermute | solution.py:552
  118.7 3.2 %down.1.rest_2_ = f32[32,32,128]{2,1,0:T(8,128)S(1)} custom-call(s32[2]{0:T(128)S(1)} %pad_add_fusion.place_ref, f32[1,32,64]{2,1,0:T(8,128)S(1)} %root.1.refs_0_, f32[1,32,64]{2,1,0:T(8,128)S(1)} %collective-permute-done.16.refs_1_, f32[1,32,64]{2,1,0:T(8,128)S(1)} %collective-permute-done.17.refs_2_, f32[1,32,64]{2,1,0:T(8,128)S(1)} %collective-permute-done.18.refs_3_, ...), custom_call_target="tpu_custom_call" | custom-call | flops 251658240 | bytes 1966080 | tf_op jit(solution)/shard_map/down/pallas_call | solution.py:495
  121.9 2.5 %final.1 = bf16[32,8192]{1,0:T(8,128)(2,1)} custom-call(f32[32,32,128]{2,1,0:T(8,128)S(1)} %get-tuple-element.13.own_ref, bf16[64,32,128]{2,1,0:T(8,128)(2,1)S(1)} %collective-permute-done.11.rest_0_, bf16[32,32,128]{2,1,0:T(8,128)(2,1)S(1)} %collective-permute-done.12.rest_1_, f32[32,32,128]{2,1,0:T(8,128)S(1)} %down.1.rest_2_, ...), custom_call_target="tpu_custom_call" | custom-call | flops 67108864 | bytes 5000000 | tf_op jit(solution)/shard_map/final/pallas_call | solution.py:537
  (59 shorter events, 12.3 us)
Async XLA Ops:
  3.5 9.3 %collective-permute-start.3 = (bf16[32,32,128]{2,1,0:T(8,128)(2,1)S(1)}, bf16[32,32,128]{2,1,0:T(8,128)(2,1)S(1)}, u32[]{:S(2)}, u32[]{:S(2)}) collective-permute-start(bf16[32,32,128]{2,1,0:T(8,128)(2,1)S(1)} %coefs.1.refs_3_.coef_ref), channel_id=1, source_target_pairs={{0,4},{4,0},{8,12},{12,8},{16,20},{20,16},{24,28},{28,24},{1,5},{5... | collective-permute-start | bytes 786440 | tf_op jit(solution)/shard_map/ppermute | solution.py:552
  12.8 8.4 %collective-permute-start.7 = (bf16[32,32,128]{2,1,0:T(8,128)(2,1)S(1)}, bf16[32,32,128]{2,1,0:T(8,128)(2,1)S(1)}, u32[]{:S(2)}, u32[]{:S(2)}) collective-permute-start(bf16[32,32,128]{2,1,0:T(8,128)(2,1)S(1)} %collective-permute-done.3.refs_7_), channel_id=1, source_target_pairs={{0,8},{8,16},{16,24},{12,4},{20,12},{28,20},{1,9},{9,17},{17,25},{... | collective-permute-start | bytes 786440 | tf_op jit(solution)/shard_map/ppermute | solution.py:592
  16.5 9.2 %collective-permute-start.1 = (bf16[32,32,128]{2,1,0:T(8,128)(2,1)S(1)}, bf16[32,32,128]{2,1,0:T(8,128)(2,1)S(1)}, u32[]{:S(2)}, u32[]{:S(2)}) collective-permute-start(bf16[32,32,128]{2,1,0:T(8,128)(2,1)S(1)} %coefs.1.refs_3_.coef_ref), channel_id=1, source_target_pairs={{0,2},{1,3},{2,0},{3,1},{4,6},{5,7},{6,4},{7,5},{8,10},{9,11},{10,... | collective-permute-start | bytes 786440 | tf_op jit(solution)/shard_map/ppermute | solution.py:552
  18.1 7.7 %collective-permute-start = (bf16[32,32,128]{2,1,0:T(8,128)(2,1)S(1)}, bf16[32,32,128]{2,1,0:T(8,128)(2,1)S(1)}, u32[]{:S(2)}, u32[]{:S(2)}) collective-permute-start(bf16[32,32,128]{2,1,0:T(8,128)(2,1)S(1)} %coefs.1.refs_3_.coef_ref), channel_id=1, source_target_pairs={{0,1},{1,0},{2,3},{3,2},{4,5},{5,4},{6,7},{7,6},{8,9},{9,8},{10,11... | collective-permute-start | bytes 786440 | tf_op jit(solution)/shard_map/ppermute | solution.py:552
  18.1 13.3 %collective-permute-start.5 = (bf16[32,32,128]{2,1,0:T(8,128)(2,1)S(1)}, bf16[32,32,128]{2,1,0:T(8,128)(2,1)S(1)}, u32[]{:S(2)}, u32[]{:S(2)}) collective-permute-start(bf16[32,32,128]{2,1,0:T(8,128)(2,1)S(1)} %collective-permute-done.3.refs_7_), channel_id=1, source_target_pairs={{0,2},{1,3},{2,0},{3,1},{4,6},{5,7},{6,4},{7,5},{8,10},{9,11},{10,... | collective-permute-start | bytes 786440 | tf_op jit(solution)/shard_map/ppermute | solution.py:552
  21.2 13.5 %collective-permute-start.9 = (bf16[32,32,128]{2,1,0:T(8,128)(2,1)S(1)}, bf16[32,32,128]{2,1,0:T(8,128)(2,1)S(1)}, u32[]{:S(2)}, u32[]{:S(2)}) collective-permute-start(bf16[32,32,128]{2,1,0:T(8,128)(2,1)S(1)} %collective-permute-done.7.refs_11_), channel_id=1, source_target_pairs={{0,2},{1,3},{2,0},{3,1},{4,6},{5,7},{6,4},{7,5},{8,10},{9,11},{10,... | collective-permute-start | bytes 786440 | tf_op jit(solution)/shard_map/ppermute | solution.py:552
  22.7 45.1 %collective-permute-start.4 = (bf16[32,32,128]{2,1,0:T(8,128)(2,1)S(1)}, bf16[32,32,128]{2,1,0:T(8,128)(2,1)S(1)}, u32[]{:S(2)}, u32[]{:S(2)}) collective-permute-start(bf16[32,32,128]{2,1,0:T(8,128)(2,1)S(1)} %collective-permute-done.3.refs_7_), channel_id=1, source_target_pairs={{0,1},{1,0},{2,3},{3,2},{4,5},{5,4},{6,7},{7,6},{8,9},{9,8},{10,11... | collective-permute-start | bytes 786440 | tf_op jit(solution)/shard_map/ppermute | solution.py:552
  25.8 42.0 %collective-permute-start.2 = (bf16[32,32,128]{2,1,0:T(8,128)(2,1)S(1)}, bf16[32,32,128]{2,1,0:T(8,128)(2,1)S(1)}, u32[]{:S(2)}, u32[]{:S(2)}) collective-permute-start(bf16[32,32,128]{2,1,0:T(8,128)(2,1)S(1)} %collective-permute-done.1.refs_5_), channel_id=1, source_target_pairs={{0,1},{1,0},{2,3},{3,2},{4,5},{5,4},{6,7},{7,6},{8,9},{9,8},{10,11... | collective-permute-start | bytes 786440 | tf_op jit(solution)/shard_map/ppermute | solution.py:552
  25.8 42.0 %collective-permute-start.8 = (bf16[32,32,128]{2,1,0:T(8,128)(2,1)S(1)}, bf16[32,32,128]{2,1,0:T(8,128)(2,1)S(1)}, u32[]{:S(2)}, u32[]{:S(2)}) collective-permute-start(bf16[32,32,128]{2,1,0:T(8,128)(2,1)S(1)} %collective-permute-done.7.refs_11_), channel_id=1, source_target_pairs={{0,1},{1,0},{2,3},{3,2},{4,5},{5,4},{6,7},{7,6},{8,9},{9,8},{10,11... | collective-permute-start | bytes 786440 | tf_op jit(solution)/shard_map/ppermute | solution.py:552
  31.4 36.4 %collective-permute-start.6 = (bf16[32,32,128]{2,1,0:T(8,128)(2,1)S(1)}, bf16[32,32,128]{2,1,0:T(8,128)(2,1)S(1)}, u32[]{:S(2)}, u32[]{:S(2)}) collective-permute-start(bf16[32,32,128]{2,1,0:T(8,128)(2,1)S(1)} %collective-permute-done.5.refs_9_), channel_id=1, source_target_pairs={{0,1},{1,0},{2,3},{3,2},{4,5},{5,4},{6,7},{7,6},{8,9},{9,8},{10,11... | collective-permute-start | bytes 786440 | tf_op jit(solution)/shard_map/ppermute | solution.py:552
  34.7 33.1 %collective-permute-start.10 = (bf16[32,32,128]{2,1,0:T(8,128)(2,1)S(1)}, bf16[32,32,128]{2,1,0:T(8,128)(2,1)S(1)}, u32[]{:S(2)}, u32[]{:S(2)}) collective-permute-start(bf16[32,32,128]{2,1,0:T(8,128)(2,1)S(1)} %collective-permute-done.9.refs_13_), channel_id=1, source_target_pairs={{0,1},{1,0},{2,3},{3,2},{4,5},{5,4},{6,7},{7,6},{8,9},{9,8},{10,11... | collective-permute-start | bytes 786440 | tf_op jit(solution)/shard_map/ppermute | solution.py:552
  38.1 29.0 %copy-start.12 = (s32[1,1024]{1,0:T(1,128)S(1)}, s32[1,1024]{1,0:T(1,128)}, u32[]{:S(2)}) copy-start(s32[1,1024]{1,0:T(1,128)} %param.17) | copy-start | bytes 12292
  83.2 2.0 %collective-permute-start.11 = (bf16[64,32,128]{2,1,0:T(8,128)(2,1)S(1)}, bf16[64,32,128]{2,1,0:T(8,128)(2,1)S(1)}, u32[]{:S(2)}, u32[]{:S(2)}) collective-permute-start(bf16[64,32,128]{2,1,0:T(8,128)(2,1)S(1)} %get-tuple-element.14), channel_id=1, source_target_pairs={{0,1},{1,0},{2,3},{3,2},{4,5},{5,4},{6,7},{7,6},{8,9},{9,8},{10,11... | collective-permute-start | bytes 1572872 | tf_op jit(solution)/shard_map/ppermute | solution.py:552
  85.3 36.6 %collective-permute-start.12 = (bf16[32,32,128]{2,1,0:T(8,128)(2,1)S(1)}, bf16[32,32,128]{2,1,0:T(8,128)(2,1)S(1)}, u32[]{:S(2)}, u32[]{:S(2)}) collective-permute-start(bf16[32,32,128]{2,1,0:T(8,128)(2,1)S(1)} %add_convert_fusion), channel_id=1, source_target_pairs={{0,2},{1,3},{2,0},{3,1},{4,6},{5,7},{6,4},{7,5},{8,10},{9,11},{10,... | collective-permute-start | bytes 786440 | tf_op jit(solution)/shard_map/ppermute | solution.py:552
  98.3 1.9 %collective-permute-start.13 = (f32[1,32,64]{2,1,0:T(8,128)S(1)}, f32[1,32,64]{2,1,0:T(8,128)S(1)}, u32[]{:S(2)}, u32[]{:S(2)}) collective-permute-start(f32[1,32,64]{2,1,0:T(8,128)S(1)} %get-tuple-element.16.refs_0_), channel_id=1, source_target_pairs={{0,1},{1,0},{2,3},{3,2},{4,5},{5,4},{6,7},{7,6},{8,9},{9,8},{10,11... | collective-permute-start | bytes 24584 | tf_op jit(solution)/shard_map/ppermute | solution.py:552
  98.4 3.8 %collective-permute-start.14 = (f32[1,32,64]{2,1,0:T(8,128)S(1)}, f32[1,32,64]{2,1,0:T(8,128)S(1)}, u32[]{:S(2)}, u32[]{:S(2)}) collective-permute-start(f32[1,32,64]{2,1,0:T(8,128)S(1)} %get-tuple-element.16.refs_0_), channel_id=1, source_target_pairs={{0,2},{1,3},{2,0},{3,1},{4,6},{5,7},{6,4},{7,5},{8,10},{9,11},{10,... | collective-permute-start | bytes 24584 | tf_op jit(solution)/shard_map/ppermute | solution.py:552
  98.5 3.6 %collective-permute-start.15 = (f32[1,32,64]{2,1,0:T(8,128)S(1)}, f32[1,32,64]{2,1,0:T(8,128)S(1)}, u32[]{:S(2)}, u32[]{:S(2)}) collective-permute-start(f32[1,32,64]{2,1,0:T(8,128)S(1)} %get-tuple-element.16.refs_0_), channel_id=1, source_target_pairs={{0,3},{1,2},{2,1},{3,0},{4,7},{5,6},{6,5},{7,4},{8,11},{9,10},{10,... | collective-permute-start | bytes 24584 | tf_op jit(solution)/shard_map/ppermute | solution.py:552
  102.4 6.5 %collective-permute-start.16 = (f32[1,32,64]{2,1,0:T(8,128)S(1)}, f32[1,32,64]{2,1,0:T(8,128)S(1)}, u32[]{:S(2)}, u32[]{:S(2)}) collective-permute-start(f32[1,32,64]{2,1,0:T(8,128)S(1)} %root.1.refs_0_), channel_id=1, source_target_pairs={{0,4},{4,0},{8,12},{12,8},{16,20},{20,16},{24,28},{28,24},{1,5},{5... | collective-permute-start | bytes 24584 | tf_op jit(solution)/shard_map/ppermute | solution.py:552
  102.4 6.6 %collective-permute-start.17 = (f32[1,32,64]{2,1,0:T(8,128)S(1)}, f32[1,32,64]{2,1,0:T(8,128)S(1)}, u32[]{:S(2)}, u32[]{:S(2)}) collective-permute-start(f32[1,32,64]{2,1,0:T(8,128)S(1)} %root.1.refs_0_), channel_id=1, source_target_pairs={{0,8},{4,12},{8,0},{12,4},{16,24},{20,28},{24,16},{28,20},{1,9},{5... | collective-permute-start | bytes 24584 | tf_op jit(solution)/shard_map/ppermute | solution.py:552
  104.4 7.9 %collective-permute-start.18 = (f32[1,32,64]{2,1,0:T(8,128)S(1)}, f32[1,32,64]{2,1,0:T(8,128)S(1)}, u32[]{:S(2)}, u32[]{:S(2)}) collective-permute-start(f32[1,32,64]{2,1,0:T(8,128)S(1)} %root.1.refs_0_), channel_id=1, source_target_pairs={{0,12},{4,8},{8,4},{12,0},{16,28},{20,24},{24,20},{28,16},{1,13},{... | collective-permute-start | bytes 24584 | tf_op jit(solution)/shard_map/ppermute | solution.py:552
  105.9 9.7 %collective-permute-start.19 = (f32[1,32,64]{2,1,0:T(8,128)S(1)}, f32[1,32,64]{2,1,0:T(8,128)S(1)}, u32[]{:S(2)}, u32[]{:S(2)}) collective-permute-start(f32[1,32,64]{2,1,0:T(8,128)S(1)} %root.1.refs_0_), channel_id=1, source_target_pairs={{0,16},{4,20},{8,24},{12,28},{16,0},{20,4},{24,8},{28,12},{1,17},{... | collective-permute-start | bytes 24584 | tf_op jit(solution)/shard_map/ppermute | solution.py:552
  109.0 6.7 %collective-permute-start.20 = (f32[1,32,64]{2,1,0:T(8,128)S(1)}, f32[1,32,64]{2,1,0:T(8,128)S(1)}, u32[]{:S(2)}, u32[]{:S(2)}) collective-permute-start(f32[1,32,64]{2,1,0:T(8,128)S(1)} %root.1.refs_0_), channel_id=1, source_target_pairs={{0,20},{4,16},{8,28},{12,24},{16,4},{20,0},{24,12},{28,8},{1,21},{... | collective-permute-start | bytes 24584 | tf_op jit(solution)/shard_map/ppermute | solution.py:552
  109.0 6.7 %collective-permute-start.21 = (f32[1,32,64]{2,1,0:T(8,128)S(1)}, f32[1,32,64]{2,1,0:T(8,128)S(1)}, u32[]{:S(2)}, u32[]{:S(2)}) collective-permute-start(f32[1,32,64]{2,1,0:T(8,128)S(1)} %root.1.refs_0_), channel_id=1, source_target_pairs={{0,24},{4,28},{8,16},{12,20},{16,8},{20,12},{24,0},{28,4},{1,25},{... | collective-permute-start | bytes 24584 | tf_op jit(solution)/shard_map/ppermute | solution.py:552
  112.3 6.4 %collective-permute-start.22 = (f32[1,32,64]{2,1,0:T(8,128)S(1)}, f32[1,32,64]{2,1,0:T(8,128)S(1)}, u32[]{:S(2)}, u32[]{:S(2)}) collective-permute-start(f32[1,32,64]{2,1,0:T(8,128)S(1)} %root.1.refs_0_), channel_id=1, source_target_pairs={{0,28},{4,24},{8,20},{12,16},{16,12},{20,8},{24,4},{28,0},{1,29},{... | collective-permute-start | bytes 24584 | tf_op jit(solution)/shard_map/ppermute | solution.py:552
  (12 other events, 171.9 us)
